TPU v7x, 32 devices: a whole 2x2x4 slice. The times are simulated.
32 devices in a mesh: shard: 4 (over y, core), ctx: 4 (over z), tp: 2 (over x).
Axes of the slice: x: 2, y: 2, z: 4, core: 2. Of those that a mesh axis runs over, the one named last changes fastest.
Arguments:
- layer_input: bfloat16 [4, 1024, 1024], P('shard', 'ctx'), may hold values from -6 to 6
- attn_norm: bfloat16 [1024], P(('shard', 'ctx')), may hold values from 0.5 to 1.5
- w_query: bfloat16 [1024, 1024], P(('shard', 'ctx'), 'tp'), may hold values from -0.25 to 0.25
- w_key: bfloat16 [1024, 512], P(('shard', 'ctx'), 'tp'), may hold values from -0.25 to 0.25
- w_value: bfloat16 [1024, 512], P(('shard', 'ctx'), 'tp'), may hold values from -0.1875 to 0.1875
- w_out: bfloat16 [1024, 1024], P('tp', ('shard', 'ctx')), may hold values from -1.5 to 1.5
- moe_norm: bfloat16 [1024], P(('shard', 'ctx')), may hold values from 0.5 to 1.5
- expert_weights: bfloat16 [32, 3, 1024, 512], P('ctx', None, 'shard', 'tp')
- expert_ids: int32 [4, 1024, 8], P('shard', 'ctx'), may hold values from 0 to 31, as said below
- slot_ids: int32 [4, 1024, 8], P('shard', 'ctx'), may hold values from 0 to 96, as said below
- gate_values: float32 [4, 1024, 8], P('shard', 'ctx'), may hold values from 0.06 to 0.25
- piece_starts: int32 [4, 1], P('shard'), may hold values from 0 to 768, as said below
- grad_out: bfloat16 [4, 1024, 1024], P('shard', 'ctx'), may hold values from -6 to 6
Outputs:
- output: bfloat16 [4, 1024, 1024], P('shard', 'ctx')
- input_grad: bfloat16 [4, 1024, 1024], P('shard', 'ctx')
- attn_norm_grad: float32 [1024], P(('shard', 'ctx'))
- query_grad: float32 [1024, 1024], P(('shard', 'ctx'), 'tp')
- key_grad: float32 [1024, 512], P(('shard', 'ctx'), 'tp')
- value_grad: float32 [1024, 512], P(('shard', 'ctx'), 'tp')
- out_grad: float32 [1024, 1024], P('tp', ('shard', 'ctx'))
- moe_norm_grad: float32 [1024], P(('shard', 'ctx'))
- expert_grad: float32 [32, 3, 1024, 512], P('ctx', None, 'shard', 'tp')
Inputs may be any that keep to these rules, and one draw needn't show every extreme that they name: `expert_ids`: each row names 8 different experts. `slot_ids`: within each aligned group of 256 positions of a sequence, the pairs (position, k) that name an expert get slots 0, 1, 2, ... in order of position and then of k; a pair whose rank is 96 or more gets 96 and is dropped. In every group some expert is named 96 times or more, and in every sequence one expert is so in all of its groups. `piece_starts`: piece k of a sequence starts between k * 4 * 256 and k * 4 * 256 + 3 * 256; in the first sequence the first piece starts at 0 and the last at the latest start allowed; when a sequence has only one piece, that piece starts at the latest start allowed.
All inputs are finite; a program needn't handle non-finite values.
Results may differ from a plain program's by a relative error of at most 0.018.
Values may be sent and summed in bfloat16 or wider, within the bound.
No kernel may reach another device: no remote copies, remote signals or barrier semaphores. Data moves between devices by JAX's collectives and lax.ppermute only.
A program may use at most 192 MiB of HBM per device.

v0:
```python
import math

import jax
import jax.numpy as jnp
from jax import lax
from jax.sharding import PartitionSpec as P

HEAD_DIM = 64
EXPERTS = 32
TOPK = 8
PIECE = 256
CAP = 96


EPS = 1e-06
MASKED = -1e30


def rotate(values, positions, direction):
    half_dim = values.shape[-1] // 2
    frequency = 1.0 / 10000.0 ** (jnp.arange(half_dim, dtype=jnp.float32) * 2.0 / values.shape[-1])
    angles = positions.astype(jnp.float32)[:, None] * frequency[None, :]
    cosine = jnp.cos(angles)[:, None, :]
    sine_part = direction * jnp.sin(angles)[:, None, :]
    first_half = values[..., :half_dim]
    second = values[..., half_dim:]
    return jnp.concatenate(
        [first_half * cosine - second * sine_part, second * cosine + first_half * sine_part],
        axis=-1,
    )


def picture_of(positions, starts):
    inside = (positions[:, None] >= starts[None, :]) & (
        positions[:, None] < starts[None, :] + PIECE
    )
    labels = jnp.arange(1, starts.shape[0] + 1, dtype=jnp.int32)
    return jnp.sum(jnp.where(inside, labels[None, :], 0), axis=-1)


def visible(query_pos, key_pos, query_label, key_label):
    causal = key_pos[None, :] <= query_pos[:, None]
    same_piece = (query_label[:, None] == key_label[None, :]) & (query_label[:, None] > 0)
    return causal | same_piece


def expert_math(weight_set, rows_in, grads_in):
    gate_w = weight_set[:, 0]
    up_w = weight_set[:, 1]
    down_w = weight_set[:, 2]
    gate_lin = jnp.einsum("esrd,edf->esrf", rows_in, gate_w, preferred_element_type=jnp.float32)
    up_lin = jnp.einsum("esrd,edf->esrf", rows_in, up_w, preferred_element_type=jnp.float32)
    sigmoid_gate = jax.nn.sigmoid(gate_lin)
    silu_gate = gate_lin * sigmoid_gate
    hidden_act = (silu_gate * up_lin).astype(jnp.bfloat16)
    expert_out = jnp.einsum(
        "esrf,edf->esrd", hidden_act, down_w, preferred_element_type=jnp.float32
    )
    act_grad = jnp.einsum("esrd,edf->esrf", grads_in, down_w, preferred_element_type=jnp.float32)
    up_grad = (act_grad * silu_gate).astype(jnp.bfloat16)
    gate_grad = (act_grad * up_lin * sigmoid_gate * (1.0 + gate_lin * (1.0 - sigmoid_gate))).astype(
        jnp.bfloat16
    )
    input_part = jnp.einsum("esrf,edf->esrd", gate_grad, gate_w, preferred_element_type=jnp.float32)
    input_part = input_part + jnp.einsum(
        "esrf,edf->esrd", up_grad, up_w, preferred_element_type=jnp.float32
    )
    weight_grad = jnp.stack(
        [
            jnp.einsum("esrd,esrf->edf", rows_in, gate_grad, preferred_element_type=jnp.float32),
            jnp.einsum("esrd,esrf->edf", rows_in, up_grad, preferred_element_type=jnp.float32),
            jnp.einsum("esrd,esrf->edf", grads_in, hidden_act, preferred_element_type=jnp.float32),
        ],
        axis=1,
    )
    return (expert_out, input_part, weight_grad)


def local(
    layer_input,
    attn_norm,
    w_query,
    w_key,
    w_value,
    w_out,
    moe_norm,
    expert_weights,
    expert_ids,
    slot_ids,
    gate_values,
    piece_starts,
    grad_out,
):
    sequences, tokens_here, model_width = layer_input.shape
    row_count = sequences * tokens_here
    length = tokens_here * lax.axis_size("ctx")
    positions = lax.axis_index("ctx") * tokens_here + jnp.arange(tokens_here, dtype=jnp.int32)
    gain_one, query_w, key_w, value_w, out_w, gain_two = (
        lax.all_gather(attn_norm, ("shard", "ctx"), axis=0, tiled=True),
        lax.all_gather(w_query, ("shard", "ctx"), axis=0, tiled=True),
        lax.all_gather(w_key, ("shard", "ctx"), axis=0, tiled=True),
        lax.all_gather(w_value, ("shard", "ctx"), axis=0, tiled=True),
        lax.all_gather(w_out, ("shard", "ctx"), axis=1, tiled=True),
        lax.all_gather(moe_norm, ("shard", "ctx"), axis=0, tiled=True),
    )
    expert_rows = lax.all_gather(expert_weights, "shard", axis=2, tiled=True)
    gain_one = gain_one.astype(jnp.float32)
    gain_two = gain_two.astype(jnp.float32)
    head_count = query_w.shape[1] // HEAD_DIM
    key_heads = key_w.shape[1] // HEAD_DIM
    group_size = head_count // key_heads
    score_scale = HEAD_DIM ** (-0.5)
    flat_input = layer_input.astype(jnp.float32).reshape(row_count, model_width)
    inverse_one = lax.rsqrt(jnp.mean(flat_input * flat_input, axis=-1, keepdims=True) + EPS)
    normed_one = (flat_input * inverse_one * gain_one).astype(jnp.bfloat16)
    query_lin = jnp.dot(normed_one, query_w, preferred_element_type=jnp.float32)
    key_lin = jnp.dot(normed_one, key_w, preferred_element_type=jnp.float32)
    value_lin = jnp.dot(normed_one, value_w, preferred_element_type=jnp.float32)
    queries = rotate(
        query_lin.reshape(sequences, tokens_here, head_count, HEAD_DIM), positions, 1.0
    ).astype(jnp.bfloat16)
    queries = queries.reshape(sequences, tokens_here, key_heads, group_size, HEAD_DIM)
    keys = rotate(
        key_lin.reshape(sequences, tokens_here, key_heads, HEAD_DIM), positions, 1.0
    ).astype(jnp.bfloat16)
    keys = keys.reshape(sequences, tokens_here, key_heads * HEAD_DIM)
    values = value_lin.astype(jnp.bfloat16).reshape(sequences, tokens_here, key_heads * HEAD_DIM)
    all_keys, all_values = (
        lax.all_gather(keys, "ctx", axis=1, tiled=True),
        lax.all_gather(values, "ctx", axis=1, tiled=True),
    )
    label_of = jax.vmap(picture_of, (None, 0))
    query_label = label_of(positions, piece_starts)
    key_span = math.gcd(length, max(tokens_here, 512))
    block_count = length // key_span

    def block_scores(block_index):
        block_start = block_index * key_span
        key_pos = block_start + jnp.arange(key_span, dtype=jnp.int32)
        visible_mask = jax.vmap(visible, (None, None, 0, 0))(
            positions, key_pos, query_label, label_of(key_pos, piece_starts)
        )
        key_block = lax.dynamic_slice_in_dim(all_keys, block_start, key_span, 1).reshape(
            sequences, key_span, key_heads, HEAD_DIM
        )
        value_block = lax.dynamic_slice_in_dim(all_values, block_start, key_span, 1).reshape(
            sequences, key_span, key_heads, HEAD_DIM
        )
        scores = (
            jnp.einsum("sqhgd,skhd->shgqk", queries, key_block, preferred_element_type=jnp.float32)
            * score_scale
        )
        scores = jnp.where(visible_mask[:, None, None], scores, MASKED)
        return (scores, key_block, value_block)

    stat_shape = (sequences, key_heads, group_size, tokens_here)

    def stats_step(state_pair, block_index):
        row_max, row_sum = state_pair
        scores = block_scores(block_index)[0]
        new_max = jnp.maximum(row_max, jnp.max(scores, axis=-1))
        row_sum = row_sum * jnp.exp(row_max - new_max) + jnp.sum(
            jnp.exp(scores - new_max[..., None]), axis=-1
        )
        return ((new_max, row_sum), None)

    (row_max, row_sum), unused = lax.scan(
        stats_step,
        (jnp.full(stat_shape, MASKED, jnp.float32), jnp.zeros(stat_shape, jnp.float32)),
        jnp.arange(block_count),
    )

    def output_step(acc_pair, block_index):
        accumulated, exact_sum = acc_pair
        scores, key_block, value_block = block_scores(block_index)
        probability = jnp.exp(scores - row_max[..., None]) / row_sum[..., None]
        accumulated = accumulated + jnp.einsum(
            "shgqk,skhd->sqhgd",
            probability.astype(jnp.bfloat16),
            value_block,
            preferred_element_type=jnp.float32,
        )
        exact_sum = exact_sum + jnp.einsum(
            "shgqk,skhd->sqhgd",
            probability,
            value_block.astype(jnp.float32),
            precision=lax.Precision.HIGHEST,
        )
        return ((accumulated, exact_sum), None)

    query_shape = (sequences, tokens_here, key_heads, group_size, HEAD_DIM)
    (attended, exact_attended), unused = lax.scan(
        output_step,
        (jnp.zeros(query_shape, jnp.float32), jnp.zeros(query_shape, jnp.float32)),
        jnp.arange(block_count),
    )
    mixed = attended.astype(jnp.bfloat16).reshape(row_count, head_count * HEAD_DIM)
    attention = lax.psum(jnp.dot(mixed, out_w, preferred_element_type=jnp.float32), "tp")
    residual = flat_input + attention
    inverse_two = lax.rsqrt(jnp.mean(residual * residual, axis=-1, keepdims=True) + EPS)
    normed_two = (residual * inverse_two * gain_two).astype(jnp.bfloat16)
    slot_rows = sequences * CAP
    capacity_rows = EXPERTS * slot_rows
    seq_offset = jnp.arange(sequences, dtype=jnp.int32)[:, None, None] * CAP
    slot_index = jnp.where(
        slot_ids < CAP, expert_ids * slot_rows + seq_offset + slot_ids, capacity_rows
    ).reshape(-1)
    owner_row = jnp.repeat(jnp.arange(row_count, dtype=jnp.int32), TOPK)
    source = (
        jnp.full((capacity_rows + 1,), row_count, jnp.int32)
        .at[slot_index]
        .set(owner_row)[:capacity_rows]
    )
    slot_gate = (
        jnp.zeros((capacity_rows + 1,), jnp.float32)
        .at[slot_index]
        .set(gate_values.reshape(-1))[:capacity_rows]
    )
    padded_input = jnp.concatenate([normed_two, jnp.zeros((1, model_width), jnp.bfloat16)], axis=0)
    padded_cotangent = jnp.concatenate(
        [grad_out.reshape(row_count, model_width), jnp.zeros((1, model_width), jnp.bfloat16)],
        axis=0,
    )
    dispatched = padded_input[source].reshape(EXPERTS, 1, slot_rows, model_width)
    out_grads = (slot_gate[:, None] * padded_cotangent[source].astype(jnp.float32)).astype(
        jnp.bfloat16
    )
    out_grads = out_grads.reshape(EXPERTS, 1, slot_rows, model_width)
    rows_in, grads_in = (
        lax.all_to_all(dispatched, "ctx", split_axis=0, concat_axis=1, tiled=True),
        lax.all_to_all(out_grads, "ctx", split_axis=0, concat_axis=1, tiled=True),
    )
    expert_part, input_part, local_grad = expert_math(expert_rows, rows_in, grads_in)
    expert_back, input_back = (
        lax.all_to_all(expert_part, "ctx", split_axis=1, concat_axis=0, tiled=True),
        lax.all_to_all(input_part, "ctx", split_axis=1, concat_axis=0, tiled=True),
    )
    expert_grad = lax.psum_scatter(
        local_grad.astype(jnp.bfloat16), "shard", scatter_dimension=2, tiled=True
    ).astype(jnp.float32)
    zero_row = jnp.zeros((1, model_width), jnp.float32)
    padded_out = jnp.concatenate(
        [expert_back.reshape(capacity_rows, model_width), zero_row], axis=0
    )
    padded_back = jnp.concatenate(
        [input_back.reshape(capacity_rows, model_width), zero_row], axis=0
    )
    gate_column = gate_values.reshape(row_count, TOPK, 1)
    moe_part = jnp.sum(
        gate_column * padded_out[slot_index].reshape(row_count, TOPK, model_width), axis=1
    )
    normed_part = jnp.sum(padded_back[slot_index].reshape(row_count, TOPK, model_width), axis=1)
    moe_sum, normed_two_grad = lax.psum((moe_part, normed_part), "tp")
    output = (residual + moe_sum).astype(jnp.bfloat16).reshape(sequences, tokens_here, model_width)
    cotangent = grad_out.astype(jnp.float32).reshape(row_count, model_width)
    scaled_two = gain_two * normed_two_grad
    residual_grad = (
        cotangent
        + inverse_two * scaled_two
        - residual * inverse_two**3 * jnp.mean(scaled_two * residual, axis=-1, keepdims=True)
    )
    gain_two_grad = jnp.sum(normed_two_grad * residual * inverse_two, axis=0)
    branch_grad = residual_grad.astype(jnp.bfloat16)
    out_w_grad = jnp.einsum("rc,rd->cd", mixed, branch_grad, preferred_element_type=jnp.float32)
    mixed_grad = jnp.einsum(
        "rd,cd->rc", branch_grad, out_w, preferred_element_type=jnp.float32
    ).astype(jnp.bfloat16)
    mixed_grad = mixed_grad.reshape(query_shape)
    row_delta = jnp.transpose(
        jnp.sum(mixed_grad.astype(jnp.float32) * exact_attended, axis=-1), (0, 2, 3, 1)
    )

    def grad_step(grad_state, block_index):
        query_acc, key_acc, value_acc = grad_state
        scores, key_block, value_block = block_scores(block_index)
        probability = jnp.exp(scores - row_max[..., None]) / row_sum[..., None]
        prob_grad = jnp.einsum(
            "sqhgd,skhd->shgqk", mixed_grad, value_block, preferred_element_type=jnp.float32
        )
        score_grad = (probability * (prob_grad - row_delta[..., None])).astype(jnp.bfloat16)
        query_acc = query_acc + jnp.einsum(
            "shgqk,skhd->sqhgd", score_grad, key_block, preferred_element_type=jnp.float32
        )
        key_part = (
            jnp.einsum("shgqk,sqhgd->skhd", score_grad, queries, preferred_element_type=jnp.float32)
            * score_scale
        )
        value_part = jnp.einsum(
            "shgqk,sqhgd->skhd",
            probability.astype(jnp.bfloat16),
            mixed_grad,
            preferred_element_type=jnp.float32,
        )
        block_start = block_index * key_span
        key_acc = lax.dynamic_update_slice_in_dim(
            key_acc, key_part.reshape(sequences, key_span, key_heads * HEAD_DIM), block_start, 1
        )
        value_acc = lax.dynamic_update_slice_in_dim(
            value_acc, value_part.reshape(sequences, key_span, key_heads * HEAD_DIM), block_start, 1
        )
        return ((query_acc, key_acc, value_acc), None)

    key_shape = (sequences, length, key_heads * HEAD_DIM)
    grad_start = (
        jnp.zeros(query_shape, jnp.float32),
        jnp.zeros(key_shape, jnp.float32),
        jnp.zeros(key_shape, jnp.float32),
    )
    (query_acc, key_acc, value_acc), unused = lax.scan(
        grad_step, grad_start, jnp.arange(block_count)
    )
    key_sum, value_sum = (
        lax.psum_scatter(key_acc, "ctx", scatter_dimension=1, tiled=True),
        lax.psum_scatter(value_acc, "ctx", scatter_dimension=1, tiled=True),
    )
    query_lin_grad = rotate(
        (query_acc * score_scale).reshape(sequences, tokens_here, head_count, HEAD_DIM),
        positions,
        -1.0,
    )
    query_lin_grad = query_lin_grad.astype(jnp.bfloat16).reshape(row_count, head_count * HEAD_DIM)
    key_lin_grad = rotate(
        key_sum.reshape(sequences, tokens_here, key_heads, HEAD_DIM), positions, -1.0
    )
    key_lin_grad = key_lin_grad.astype(jnp.bfloat16).reshape(row_count, key_heads * HEAD_DIM)
    value_lin_grad = value_sum.astype(jnp.bfloat16).reshape(row_count, key_heads * HEAD_DIM)
    query_w_grad = jnp.einsum(
        "rd,rc->dc", normed_one, query_lin_grad, preferred_element_type=jnp.float32
    )
    key_w_grad = jnp.einsum(
        "rd,rc->dc", normed_one, key_lin_grad, preferred_element_type=jnp.float32
    )
    value_w_grad = jnp.einsum(
        "rd,rc->dc", normed_one, value_lin_grad, preferred_element_type=jnp.float32
    )
    normed_one_part = jnp.einsum(
        "rc,dc->rd", query_lin_grad, query_w, preferred_element_type=jnp.float32
    )
    normed_one_part = normed_one_part + jnp.einsum(
        "rc,dc->rd", key_lin_grad, key_w, preferred_element_type=jnp.float32
    )
    normed_one_part = normed_one_part + jnp.einsum(
        "rc,dc->rd", value_lin_grad, value_w, preferred_element_type=jnp.float32
    )
    normed_one_grad = lax.psum(normed_one_part.astype(jnp.bfloat16), "tp").astype(jnp.float32)
    scaled_one = gain_one * normed_one_grad
    input_grad = (
        residual_grad
        + inverse_one * scaled_one
        - flat_input * inverse_one**3 * jnp.mean(scaled_one * flat_input, axis=-1, keepdims=True)
    )
    gain_one_grad = jnp.sum(normed_one_grad * flat_input * inverse_one, axis=0)
    attn_norm_grad, query_grad, key_grad, value_grad, out_grad, moe_norm_grad = (
        lax.psum_scatter(gain_one_grad, ("shard", "ctx"), scatter_dimension=0, tiled=True),
        lax.psum_scatter(query_w_grad, ("shard", "ctx"), scatter_dimension=0, tiled=True),
        lax.psum_scatter(key_w_grad, ("shard", "ctx"), scatter_dimension=0, tiled=True),
        lax.psum_scatter(value_w_grad, ("shard", "ctx"), scatter_dimension=0, tiled=True),
        lax.psum_scatter(out_w_grad, ("shard", "ctx"), scatter_dimension=1, tiled=True),
        lax.psum_scatter(gain_two_grad, ("shard", "ctx"), scatter_dimension=0, tiled=True),
    )
    return (
        output,
        input_grad.astype(jnp.bfloat16).reshape(sequences, tokens_here, model_width),
        attn_norm_grad,
        query_grad,
        key_grad,
        value_grad,
        out_grad,
        moe_norm_grad,
        expert_grad,
    )


def solution(mesh):
    in_specs = (
        P("shard", "ctx", None),
        P(("shard", "ctx")),
        P(("shard", "ctx"), "tp"),
        P(("shard", "ctx"), "tp"),
        P(("shard", "ctx"), "tp"),
        P("tp", ("shard", "ctx")),
        P(("shard", "ctx")),
        P("ctx", None, "shard", "tp"),
        P("shard", "ctx", None),
        P("shard", "ctx", None),
        P("shard", "ctx", None),
        P("shard", None),
        P("shard", "ctx", None),
    )
    out_specs = (
        P("shard", "ctx", None),
        P("shard", "ctx", None),
        P(("shard", "ctx")),
        P(("shard", "ctx"), "tp"),
        P(("shard", "ctx"), "tp"),
        P(("shard", "ctx"), "tp"),
        P("tp", ("shard", "ctx")),
        P(("shard", "ctx")),
        P("ctx", None, "shard", "tp"),
    )
    return jax.shard_map(local, mesh=mesh, in_specs=in_specs, out_specs=out_specs, check_vma=False)
```

profile of v0, /device:TPU:0, one launch (start us, length us, event | category | flops | bytes accessed | tf_op | source)
XLA Modules:
  0.0 1700.1 jit_solution(17182687819154339258)
XLA Ops:
  13.3 35.4 %all-reduce.10 = (bf16[1024]{0:T(1024)(128)(2,1)S(1)}, bf16[1024]{0:T(1024)(128)(2,1)S(1)}) all-reduce(bf16[1024]{0:T(1024)(128)(2,1)S(1)} %dynamic-update-slice, bf16[1024]{0:T(1024)(128)(2,1)S(1)} %dynamic-update-slice.1), channel_id=1, replica_groups=mesh['shard'=4,'ctx'=4,'tp'=2] {'shard','ctx'}, use_global_device_ids=true, to_apply=%add.4 | all-reduce | flops 2048 | bytes 8192
  50.5 34.0 %all_gather.30 = bf16[1024,256]{1,0:T(8,128)(2,1)S(1)} all-gather(bf16[64,256]{1,0:T(8,128)(2,1)} %param.22), channel_id=1, replica_groups=mesh['shard'=4,'ctx'=4,'tp'=2] {'shard','ctx'}, dimensions={0}, use_global_device_ids=true | all-gather | bytes 557056 | tf_op jit(solution)/shard_map/all_gather | solution.py:101
  87.1 15.2 all_gather.31
  103.0 34.8 %all_gather.28 = bf16[1024,256]{1,0:T(8,128)(2,1)S(1)} all-gather(bf16[64,256]{1,0:T(8,128)(2,1)S(1)} %copy-done.46), channel_id=1, replica_groups=mesh['shard'=4,'ctx'=4,'tp'=2] {'shard','ctx'}, dimensions={0}, use_global_device_ids=true | all-gather | bytes 557056 | tf_op jit(solution)/shard_map/all_gather | solution.py:102
  138.9 15.5 all-gather
  159.5 17.6 %while.50 = (s32[]{:T(128)}, f32[1,4,2,256]{3,2,1,0:T(2,128)S(1)}, f32[1,4,2,256]{3,2,1,0:T(2,128)S(1)}, s32[2]{0:T(128)S(1)}, s32[1,1]{1,0:T(1,128)}, /*index=5...) while((s32[]{:T(128)}, f32[1,4,2,256]{3,2,1,0:T(2,128)S(1)}, ...), condition=%wide.region_4.5_spmd.clone.clone.clone, body=%wide.region_1.4_spmd.clone.clone.clone.sunk | while | flops 142096640 | bytes 9950962 | solution.py:167
  177.1 23.7 %while.51 = (s32[]{:T(128)}, f32[1,256,4,2,64]{1,4,3,2,0:T(8,128)S(1)}, f32[1,256,4,2,64]{1,4,3,2,0:T(8,128)S(1)}, s32[2]{0:T(128)S(1)}, bf16[1,1024,256]{1,2,0:...) while((s32[]{:T(128)}, ...), condition=%wide.region_6.7_spmd.clone.clone.clone, body=%wide.region_5.6_spmd.clone.clone.clone.sunk | while | flops 1080037632 | bytes 33847076 | solution.py:192
  216.5 27.4 %all-reduce.15.cloned.1.call-done = f32[256,1024]{1,0:T(8,128)} async-done(((f32[256,1024]{1,0:T(8,128)}), f32[256,1024]{1,0:T(8,128)}) %all-reduce.15.cloned.1.call-update) | async-done | bytes 1048592 | tf_op jit(solution)/shard_map/psum | solution.py:198
  266.5 14.0 gather_fusion.2
  295.3 109.5 %all-to-all-done = bf16[32,1,96,1024]{3,2,1,0:T(8,128)(2,1)} async-done(((bf16[32,1,96,1024]{3,2,1,0:T(8,128)(2,1)}), bf16[32,1,96,1024]{3,2,1,0:T(8,128)(2,1)}, u32[]{:S(2)}, u32[]{:S(2)}) %all-to-all-start) | async-done | bytes 6291488 | tf_op jit(solution)/shard_map/all_to_all | solution.py:230
  425.1 122.7 %all-to-all-done.2 = bf16[32,1,96,1024]{3,2,1,0:T(8,128)(2,1)} async-done(((bf16[32,1,96,1024]{3,2,1,0:T(8,128)(2,1)}), bf16[32,1,96,1024]{3,2,1,0:T(8,128)(2,1)}, u32[]{:S(2)}, u32[]{:S(2)}) %all-to-all-start.2) | async-done | bytes 6291488 | tf_op jit(solution)/shard_map/all_to_all | solution.py:231
  599.0 263.9 %all-to-all-done.3 = f32[8,4,96,1024]{3,2,0,1:T(8,128)} async-done(((f32[8,4,96,1024]{3,2,0,1:T(8,128)}), f32[8,4,96,1024]{3,2,0,1:T(8,128)}, u32[]{:S(2)}, u32[]{:S(2)}) %all-to-all-start.3) | async-done | bytes 12582944 | tf_op jit(solution)/shard_map/all_to_all | solution.py:236
  881.3 16.3 gather_fusion.3
  897.6 244.1 %all-to-all-done.1 = f32[8,4,96,1024]{3,2,0,1:T(8,128)} async-done(((f32[8,4,96,1024]{3,2,0,1:T(8,128)}), f32[8,4,96,1024]{3,2,0,1:T(8,128)}, u32[]{:S(2)}, u32[]{:S(2)}) %all-to-all-start.1) | async-done | bytes 12582944 | tf_op jit(solution)/shard_map/all_to_all | solution.py:235
  1153.6 16.3 gather_fusion.1
  1179.8 61.1 %all-reduce.19.cloned.1.call-done = (f32[256,1024]{1,0:T(8,128)}, f32[256,1024]{1,0:T(8,128)}) async-done(((f32[256,1024]{1,0:T(8,128)}, f32[256,1024]{1,0:T(8,128)}), (f32[256,1024]{1,0:T(8,128)}, f32[256,1024]{1,0:T(8,128)})) %all-reduce.19.cloned.1.call-update) | async-done | bytes 2097168 | tf_op jit(solution)/shard_map/psum | solution.py:253
  1250.3 22.8 %while.52 = (s32[]{:T(128)}, f32[1,256,4,2,64]{1,4,3,2,0:T(8,128)}, f32[1,1024,256]{1,2,0:T(8,128)}, f32[1,1024,256]{1,2,0:T(8,128)}, s32[2]{0:T(128)S(1)}, /*in...) while((s32[]{:T(128)}, f32[1,256,4,2,64]{1,4,3,2,0:T(8,128)}, ...), condition=%wide.region_18.19_spmd.clone.clone.clone, body=%wide.region_17.18_spmd.clone.clone.clone.sunk | while | flops 680399616 | bytes 43030428 | solution.py:309
  1301.8 26.7 %reduce-scatter.10.cloned.1.call-done = f32[1,256,256]{1,2,0:T(8,128)} async-done(((f32[1,1024,256]{1,2,0:T(8,128)}), f32[1,256,256]{1,2,0:T(8,128)}) %reduce-scatter.10.cloned.1.call-update) | async-done | bytes 262160 | tf_op jit(solution)/shard_map/reduce_scatter | solution.py:314
  1360.1 34.8 %all-reduce.8 = (f32[1024]{0:T(1024)S(1)}, f32[1024]{0:T(1024)S(1)}) all-reduce(f32[1024]{0:T(1024)S(1)} %get-tuple-element.856, f32[1024]{0:T(1024)S(1)} %get-tuple-element.854), channel_id=5, replica_groups=mesh['shard'=4,'ctx'=4,'tp'=2] {'shard','ctx'}, use_global_device_ids=true, to_apply=%region_24.25.clone | all-reduce | flops 2048 | bytes 16384
  1398.2 41.3 %reduce-scatter.20.cloned.1.call-done = bf16[8,3,256,256]{3,2,0,1:T(8,128)(2,1)} async-done(((bf16[8,3,1024,256]{3,2,0,1:T(8,128)(2,1)}), bf16[8,3,256,256]{3,2,0,1:T(8,128)(2,1)}) %reduce-scatter.20.cloned.1.call-update) | async-done | bytes 3145744 | tf_op jit(solution)/shard_map/reduce_scatter | solution.py:238
  1444.9 60.7 %reduce-scatter.18.cloned.1.call-done = f32[512,64]{0,1:T(8,128)} async-done(((f32[512,1024]{0,1:T(8,128)}), f32[512,64]{0,1:T(8,128)}) %reduce-scatter.18.cloned.1.call-update) | async-done | bytes 131088 | tf_op jit(solution)/shard_map/reduce_scatter | solution.py:358
  1505.6 64.9 %reduce-scatter.12.cloned.1.call-done = f32[64,512]{1,0:T(8,128)} async-done(((f32[1024,512]{1,0:T(8,128)}), f32[64,512]{1,0:T(8,128)}) %reduce-scatter.12.cloned.1.call-update) | async-done | bytes 131088 | tf_op jit(solution)/shard_map/reduce_scatter | solution.py:355
  1570.5 61.1 %reduce-scatter.14.cloned.1.call-done = f32[64,256]{1,0:T(8,128)} async-done(((f32[1024,256]{1,0:T(8,128)}), f32[64,256]{1,0:T(8,128)}) %reduce-scatter.14.cloned.1.call-update) | async-done | bytes 65552 | tf_op jit(solution)/shard_map/reduce_scatter | solution.py:356
  1631.6 60.7 %reduce-scatter.16.cloned.1.call-done = f32[64,256]{1,0:T(8,128)} async-done(((f32[1024,256]{1,0:T(8,128)}), f32[64,256]{1,0:T(8,128)}) %reduce-scatter.16.cloned.1.call-update) | async-done | bytes 65552 | tf_op jit(solution)/shard_map/reduce_scatter | solution.py:357
  (322 shorter events, 316.6 us)
Async XLA Ops:
  8.0 130.5 %copy-start.5 = (bf16[1,256,1024]{2,1,0:T(8,128)(2,1)S(1)}, bf16[1,256,1024]{2,1,0:T(8,128)(2,1)}, u32[]{:S(2)}) copy-start(bf16[1,256,1024]{2,1,0:T(8,128)(2,1)} %param.19) | copy-start | bytes 1572868
  8.0 94.9 %copy-start.46 = (bf16[64,256]{1,0:T(8,128)(2,1)S(1)}, bf16[64,256]{1,0:T(8,128)(2,1)}, u32[]{:S(2)}) copy-start(bf16[64,256]{1,0:T(8,128)(2,1)} %param.23) | copy-start | bytes 98308
  8.0 147.3 %all-gather.5.cloned.1.call-start = ((), (), s32[]{:S(2)}) async-start(), calls=%async_computation.11 | async-start | bytes 1114112 | tf_op jit(solution)/shard_map/all_gather | solution.py:100
  8.8 192.1 %all-gather.7.cloned.1.call-start = ((), (), s32[]{:S(2)}) async-start(), calls=%async_computation.12 | async-start | bytes 1114112 | tf_op jit(solution)/shard_map/all_gather | solution.py:103
  9.5 234.4 %all-reduce.15.cloned.1.call-start = ((), (), s32[]{:S(2)}) async-start(), calls=%async_computation.13 | async-start | bytes 2097152 | tf_op jit(solution)/shard_map/psum | solution.py:198
  48.7 108.9 %copy-start.40 = (f32[1024]{0:T(1024)}, f32[1024]{0:T(1024)S(1)}, u32[]{:S(2)}) copy-start(f32[1024]{0:T(1024)S(1)} %convert_element_type.188) | copy-start | bytes 12292
  50.5 107.1 %copy-start.44 = (f32[256]{0:T(256)}, f32[256]{0:T(256)S(1)}, u32[]{:S(2)}) copy-start(f32[256]{0:T(256)S(1)} %get-tuple-element.977) | copy-start | bytes 3076
  85.6 73.8 %copy-start.35 = (f32[256,32]{0,1:T(8,128)}, f32[256,32]{0,1:T(8,128)S(1)}, u32[]{:S(2)}) copy-start(f32[256,32]{0,1:T(8,128)S(1)} %get-tuple-element.975) | copy-start | bytes 98308
  204.1 206.1 %all-gather.9.cloned.1.call-start = ((), (), s32[]{:S(2)}) async-start(), calls=%async_computation.14 | async-start | bytes 15728640 | tf_op jit(solution)/shard_map/all_gather | solution.py:106
  260.5 144.3 %all-to-all-start = ((bf16[32,1,96,1024]{3,2,1,0:T(8,128)(2,1)}), bf16[32,1,96,1024]{3,2,1,0:T(8,128)(2,1)}, u32[]{:S(2)}, u32[]{:S(2)}) async-start(bf16[32,1,96,1024]{3,2,1,0:T(8,128)(2,1)} %bitcast.492), calls=%async_computation | async-start | bytes 12582912 | tf_op jit(solution)/shard_map/all_to_all | solution.py:230
  404.8 143.0 %all-to-all-start.2 = ((bf16[32,1,96,1024]{3,2,1,0:T(8,128)(2,1)}), bf16[32,1,96,1024]{3,2,1,0:T(8,128)(2,1)}, u32[]{:S(2)}, u32[]{:S(2)}) async-start(bf16[32,1,96,1024]{3,2,1,0:T(8,128)(2,1)} %fusion.64), calls=%async_computation.2 | async-start | bytes 12582912 | tf_op jit(solution)/shard_map/all_to_all | solution.py:231
  583.9 279.0 %all-to-all-start.3 = ((f32[8,4,96,1024]{3,2,0,1:T(8,128)}), f32[8,4,96,1024]{3,2,0,1:T(8,128)}, u32[]{:S(2)}, u32[]{:S(2)}) async-start(f32[8,4,96,1024]{3,2,0,1:T(8,128)} %copy.72), calls=%async_computation.3 | async-start | bytes 25165824 | tf_op jit(solution)/shard_map/all_to_all | solution.py:236
  862.9 278.8 %all-to-all-start.1 = ((f32[8,4,96,1024]{3,2,0,1:T(8,128)}), f32[8,4,96,1024]{3,2,0,1:T(8,128)}, u32[]{:S(2)}, u32[]{:S(2)}) async-start(f32[8,4,96,1024]{3,2,0,1:T(8,128)} %fusion.85), calls=%async_computation.1 | async-start | bytes 25165824 | tf_op jit(solution)/shard_map/all_to_all | solution.py:235
  869.2 371.7 %all-reduce.19.cloned.1.call-start = ((), (), s32[]{:S(2)}) async-start(), calls=%async_computation.23 | async-start | bytes 4194304 | tf_op jit(solution)/shard_map/psum | solution.py:253
  1169.8 71.1 %copy-start.43 = (f32[1024]{0:T(1024)S(1)}, f32[1024]{0:T(1024)}, u32[]{:S(2)}) copy-start(f32[1024]{0:T(1024)} %copy-done.42) | copy-start | bytes 12292
  1169.8 71.1 %copy-start.49 = (f32[256]{0:T(256)S(1)}, f32[256]{0:T(256)}, u32[]{:S(2)}) copy-start(f32[256]{0:T(256)} %copy-done.48) | copy-start | bytes 3076
  1179.5 120.9 %reduce-scatter.8.cloned.1.call-start = ((), (), s32[]{:S(2)}) async-start(), calls=%async_computation.15 | async-start | bytes 1310720 | tf_op jit(solution)/shard_map/reduce_scatter | solution.py:313
  1273.1 55.4 %reduce-scatter.10.cloned.1.call-start = ((), (), s32[]{:S(2)}) async-start(), calls=%async_computation.16 | async-start | bytes 1310720 | tf_op jit(solution)/shard_map/reduce_scatter | solution.py:314
  1288.7 70.0 %all-reduce.17.cloned.1.call-start = ((), (), s32[]{:S(2)}) async-start(), calls=%async_computation.17 | async-start | bytes 1048576 | tf_op jit(solution)/shard_map/psum | solution.py:345
  1330.7 108.9 %reduce-scatter.20.cloned.1.call-start = ((), (), s32[]{:S(2)}) async-start(), calls=%async_computation.22 | async-start | bytes 15728640 | tf_op jit(solution)/shard_map/reduce_scatter | solution.py:238
  1341.3 164.3 %reduce-scatter.18.cloned.1.call-start = ((), (), s32[]{:S(2)}) async-start(), calls=%async_computation.21 | async-start | bytes 2228224 | tf_op jit(solution)/shard_map/reduce_scatter | solution.py:358
  1344.4 226.1 %reduce-scatter.12.cloned.1.call-start = ((), (), s32[]{:S(2)}) async-start(), calls=%async_computation.18 | async-start | bytes 2228224 | tf_op jit(solution)/shard_map/reduce_scatter | solution.py:355
  1346.4 285.2 %reduce-scatter.14.cloned.1.call-start = ((), (), s32[]{:S(2)}) async-start(), calls=%async_computation.19 | async-start | bytes 1114112 | tf_op jit(solution)/shard_map/reduce_scatter | solution.py:356
  1347.9 344.4 %reduce-scatter.16.cloned.1.call-start = ((), (), s32[]{:S(2)}) async-start(), calls=%async_computation.20 | async-start | bytes 1114112 | tf_op jit(solution)/shard_map/reduce_scatter | solution.py:357
  (52 other events, 524.3 us)
Sparse Core Ops, SparseCore 0:
  11.1 40.6 all-gather.4
  54.0 37.2 all-gather.6
  204.2 39.6 all-reduce.14
  1179.7 61.2 all-reduce.18
  1273.2 27.1 reduce-scatter.7
  1302.7 25.8 reduce-scatter.9
  1331.4 27.2 all-reduce.16
Sparse Core Ops, SparseCore 1:
  208.1 81.6 all-gather.8
  1341.3 98.1 reduce-scatter.19
  1444.2 61.3 reduce-scatter.17
  1509.9 60.5 reduce-scatter.11
  1575.1 56.4 reduce-scatter.13
  1635.8 56.4 reduce-scatter.15
where the time goes:
time: 1710 us; the launch traced here: 1700 us
  waiting for transfers between devices  1160 us (68%)
  blocking collectives  170 us (10%)
  local copies, waits for them, and re-layouts  149 us (9%)
  matrix products  120 us (7%)
  other arithmetic  56.2 us (3%)
  starting transfers between devices  25.1 us (1%)
  between operations  18.9 us (1%)
    all_to_all x1, waiting for transfers between devices, local(): lax.all_to_all(input_part, 'ctx', split_axis=1, concat_axis=0, tiled=True)  264 us
    all_to_all x1, waiting for transfers between devices, local(): lax.all_to_all(expert_part, 'ctx', split_axis=1, concat_axis=0, tiled=True)  244 us
    all_to_all x1, waiting for transfers between devices, local(): lax.all_to_all(out_grads, 'ctx', split_axis=0, concat_axis=1, tiled=True)  123 us
    all_to_all x1, waiting for transfers between devices, local(): lax.all_to_all(dispatched, 'ctx', split_axis=0, concat_axis=1, tiled=True)  109 us
    unnamed x2, blocking collectives  70.1 us
    reduce_scatter x1, waiting for transfers between devices, local(): lax.psum_scatter(query_w_grad, ('shard', 'ctx'), scatter_dimension=0, til...  64.9 us
    reduce_scatter x1, waiting for transfers between devices, local(): lax.psum_scatter(key_w_grad, ('shard', 'ctx'), scatter_dimension=0, tiled...  61.1 us
    psum x1, waiting for transfers between devices, local(): moe_sum, normed_two_grad = lax.psum((moe_part, normed_part), 'tp')  61.1 us
  transfers between devices with their start and end apart: 17, of which 14 were waited for; matrix products, arithmetic and copies ran while one was open for 12% of the time, Pallas kernels for 0%

commit v1 on v0

v1 whole, which is shorter than its diff:
```python
import functools

import jax
import jax.numpy as jnp
from jax import lax
from jax.experimental import pallas as pl
from jax.experimental.pallas import tpu as pltpu
from jax.sharding import PartitionSpec as P

HEAD_DIM = 64
EXPERTS = 32
TOPK = 8
PIECE = 256
CAP = 96
EPS = 1e-06
MASKED = -1e30
LANES = 128
F32 = jnp.float32
BF16 = jnp.bfloat16


def swap(value, axis, distance):
    size = lax.axis_size(axis)
    return lax.ppermute(value, axis, [(i, i ^ distance) for i in range(size)])


def spread(value, axis):
    size = lax.axis_size(axis)
    copies = jnp.broadcast_to(value[None], (size,) + value.shape)
    return lax.all_to_all(copies, axis, 0, 0, tiled=True)


def dot_nn(a, b):
    return lax.dot_general(a, b, (((1,), (0,)), ((), ())), preferred_element_type=F32)


def dot_nt(a, b):
    return lax.dot_general(a, b, (((1,), (1,)), ((), ())), preferred_element_type=F32)


def dot_tn(a, b):
    return lax.dot_general(a, b, (((0,), (0,)), ((), ())), preferred_element_type=F32)


def cost(flops, moved, special=0):
    return pl.CostEstimate(flops=int(flops), bytes_accessed=int(moved), transcendentals=int(special))


def params(megabytes=56):
    return pltpu.CompilerParams(vmem_limit_bytes=megabytes * 1024 * 1024)


def sds(shape, dtype):
    return jax.ShapeDtypeStruct(shape, dtype)


def whole(shape):
    return pl.BlockSpec(shape, lambda *_: (0,) * len(shape))


def turn(value, cosine, sine):
    lane = lax.broadcasted_iota(jnp.int32, (value.shape[0], LANES), 1) % HEAD_DIM
    first = lane < HEAD_DIM // 2
    parts = []
    for j in range(value.shape[1] // LANES):
        chunk = value[:, j * LANES : (j + 1) * LANES]
        partner = jnp.where(
            first,
            pltpu.roll(chunk, LANES - HEAD_DIM // 2, 1),
            pltpu.roll(chunk, HEAD_DIM // 2, 1),
        )
        parts.append(chunk * cosine + partner * sine)
    return parts[0] if len(parts) == 1 else jnp.concatenate(parts, axis=1)


def own_first(ref, scalars, half):
    own = scalars[2] * half
    other = (1 - scalars[2]) * half
    return jnp.concatenate(
        [
            ref[pl.ds(pl.multiple_of(own, half), half)],
            ref[pl.ds(pl.multiple_of(other, half), half)],
        ],
        axis=0,
    )


def columns(scalars, p, width):
    return pl.ds(pl.multiple_of((scalars[0] ^ p) * width, width), width)


def front(scalars, layer_input, pieces, cos_table, sin_table, widths):
    tokens, model = layer_input.shape
    quarter = pieces[0].shape[0]
    q_width, kv_width = widths
    heads = q_width + 2 * kv_width
    half = tokens // 2
    count = len(pieces)

    def body(sc, x_ref, *rest):
        piece_refs = rest[:count]
        cos_ref, sin_ref, xn_ref, q_ref, kv_ref, gain_ref = rest[count:]
        values = own_first(x_ref, sc, half).astype(F32)
        rows = lax.broadcasted_iota(jnp.int32, (quarter, quarter), 0)
        diagonal = rows == lax.broadcasted_iota(jnp.int32, (quarter, quarter), 1)
        for p in range(count):
            gains = piece_refs[p][:, heads : heads + LANES].astype(F32)
            for k in range(2):
                row = jnp.sum(jnp.where(diagonal, gains[:, k : k + 1], 0.0), axis=0, keepdims=True)
                gain_ref[k : k + 1, columns(sc, p, quarter)] = row
        inverse = lax.rsqrt(jnp.mean(values * values, axis=-1, keepdims=True) + EPS)
        xn_ref[...] = (values * inverse * gain_ref[0:1, :]).astype(BF16)
        total = None
        for p in range(count):
            part = dot_nn(xn_ref[:, columns(sc, p, quarter)], piece_refs[p][:, :heads])
            total = part if total is None else total + part
        cosine, sine = cos_ref[...], sin_ref[...]
        q_ref[...] = (turn(total[:, :q_width], cosine, sine).astype(BF16) * HEAD_DIM**-0.5).astype(
            BF16
        )
        kv_ref[:, :kv_width] = turn(total[:, q_width : q_width + kv_width], cosine, sine).astype(
            BF16
        )
        kv_ref[:, kv_width:] = total[:, q_width + kv_width :].astype(BF16)

    return pl.pallas_call(
        body,
        out_shape=[
            sds((tokens, model), BF16),
            sds((tokens, q_width), BF16),
            sds((tokens, 2 * kv_width), BF16),
            sds((8, model), F32),
        ],
        grid_spec=pltpu.PrefetchScalarGridSpec(
            num_scalar_prefetch=1,
            grid=(1,),
            in_specs=[whole(layer_input.shape)]
            + [whole(p.shape) for p in pieces]
            + [whole(cos_table.shape), whole(sin_table.shape)],
            out_specs=[
                whole((tokens, model)),
                whole((tokens, q_width)),
                whole((tokens, 2 * kv_width)),
                whole((8, model)),
            ],
        ),
        compiler_params=params(),
        cost_estimate=cost(2 * tokens * model * heads, 2 * model * (2 * tokens + heads)),
        name="front",
    )(scalars, layer_input, *pieces, cos_table, sin_table)


def inside_piece(position, start):
    return (position >= start) & (position < start + PIECE)


def seen_bias(sc, query_pos, key_pos, piece_count):
    seen = key_pos <= query_pos
    for k in range(piece_count):
        start = sc[3 + k]
        seen = seen | (inside_piece(query_pos, start) & inside_piece(key_pos, start))
    return jnp.where(seen, 0.0, MASKED)


def token_position(sc, index, group, tokens):
    return group * tokens + (index ^ (sc[2] * (tokens // 2)))


def attend(scalars, queries, kv_all, out_pieces, piece_count):
    tokens, q_width = queries.shape
    length, kv2 = kv_all.shape
    kv_width = kv2 // 2
    kv_heads = kv_width // HEAD_DIM
    pair_blocks = kv_width // LANES
    count = len(out_pieces)
    quarter = out_pieces[0].shape[0]
    model = quarter * count
    half = tokens // 2

    def body(sc, q_ref, k_ref, v_ref, *rest):
        out_refs = rest[:count]
        mixed_ref, lse_ref, own_ref, send_ref, bias_ref = rest[count:]
        c = pl.program_id(0)

        @pl.when(c == 0)
        def _():
            rows = lax.broadcasted_iota(jnp.int32, (tokens, length), 0)
            cols = lax.broadcasted_iota(jnp.int32, (tokens, length), 1)
            query_pos = token_position(sc, rows, sc[1], tokens)
            key_pos = token_position(sc, cols % tokens, cols // tokens, tokens)
            bias_ref[...] = seen_bias(sc, query_pos, key_pos, piece_count)

        low = lax.broadcasted_iota(jnp.int32, (1, LANES), 1) < HEAD_DIM
        mine = low == (c % 2 == 0)
        keys = k_ref[...].astype(F32)
        keys = jnp.where(mine, keys, pltpu.roll(keys, HEAD_DIM, 1)).astype(BF16)
        vals = v_ref[...].astype(F32)
        vals = jnp.where(mine, vals, pltpu.roll(vals, HEAD_DIM, 1)).astype(BF16)
        query = q_ref[...]
        zero = jnp.zeros_like(query)
        outs, lses = [], []
        for part in (jnp.where(low, query, zero), jnp.where(low, zero, query)):
            scores = dot_nt(part, keys) + bias_ref[...]
            top = jnp.max(scores, axis=-1, keepdims=True)
            expo = jnp.exp(scores - top)
            total = jnp.sum(expo, axis=-1, keepdims=True)
            probs = expo * (1.0 / total)
            outs.append(dot_nn(probs.astype(BF16), vals))
            lses.append(top + jnp.log(total))
        mixed_ref[:, pl.ds(pl.multiple_of(c * LANES, LANES), LANES)] = jnp.where(
            low, outs[0], outs[1]
        ).astype(BF16)
        lse_ref[...] = jnp.where(low, lses[0], lses[1])

        @pl.when(c == kv_heads - 1)
        def _():
            mixed = mixed_ref[...]
            for p in range(count):
                part = dot_nt(mixed, out_refs[p][...])
                own_ref[:, columns(sc, p, quarter)] = part[:half]
                send_ref[:, columns(sc, p, quarter)] = part[half:].astype(BF16)

    return pl.pallas_call(
        body,
        out_shape=[
            sds((tokens, q_width), BF16),
            sds((tokens, kv_heads * LANES), F32),
            sds((half, model), F32),
            sds((half, model), BF16),
        ],
        grid_spec=pltpu.PrefetchScalarGridSpec(
            num_scalar_prefetch=1,
            grid=(kv_heads,),
            in_specs=[
                pl.BlockSpec((tokens, LANES), lambda c, sc: (0, c)),
                pl.BlockSpec((length, LANES), lambda c, sc: (0, c // 2)),
                pl.BlockSpec((length, LANES), lambda c, sc: (0, pair_blocks + c // 2)),
            ]
            + [whole(p.shape) for p in out_pieces],
            out_specs=[
                whole((tokens, q_width)),
                pl.BlockSpec((tokens, LANES), lambda c, sc: (0, c)),
                whole((half, model)),
                whole((half, model)),
            ],
            scratch_shapes=[pltpu.VMEM((tokens, length), F32)],
        ),
        compiler_params=params(),
        cost_estimate=cost(
            16 * tokens * length * LANES + 2 * tokens * q_width * model,
            4 * length * kv2 + 8 * tokens * model,
            2 * kv_heads * tokens * length,
        ),
        name="attend",
    )(scalars, queries, kv_all, kv_all, *out_pieces)


def second_norm(scalars, layer_input, own, received, gains):
    tokens, model = layer_input.shape
    half = tokens // 2

    def body(sc, x_ref, own_ref, rec_ref, gain_ref, res_ref, norm_ref):
        start = pl.multiple_of(sc[2] * half, half)
        residual = (
            x_ref[pl.ds(start, half)].astype(F32) + own_ref[...] + rec_ref[...].astype(F32)
        )
        inverse = lax.rsqrt(jnp.mean(residual * residual, axis=-1, keepdims=True) + EPS)
        res_ref[...] = residual
        norm_ref[...] = (residual * inverse * gain_ref[1:2, :]).astype(BF16)

    return pl.pallas_call(
        body,
        out_shape=[sds((half, model), F32), sds((half, model), BF16)],
        grid_spec=pltpu.PrefetchScalarGridSpec(
            num_scalar_prefetch=1,
            grid=(1,),
            in_specs=[
                whole((tokens, model)),
                whole((half, model)),
                whole((half, model)),
                whole((8, model)),
            ],
            out_specs=[whole((half, model)), whole((half, model))],
        ),
        compiler_params=params(),
        cost_estimate=cost(10 * half * model, 16 * half * model),
        name="second_norm",
    )(scalars, layer_input, own, received, gains)


def experts(scalars, far, rows_in, grads_in, tables, weights, first_slot):
    half, model = rows_in[0].shape
    tokens = 2 * half
    local, _, quarter, hidden = weights[0].shape
    count = len(weights)
    per_group = 2 * local
    side_rows = local * CAP

    def body(sc, *refs):
        x_refs, refs = refs[:4], refs[4:]
        g_refs, refs = refs[:4], refs[4:]
        t_refs, refs = refs[:2], refs[2:]
        w_refs, refs = refs[:count], refs[count:]
        na_ref, nb_ref, ya_ref, yb_ref, d_ref, go_ref, h_ref = refs[:7]
        st_ref, gate_ref, ns_ref, ys_ref = refs[7:]
        e = pl.program_id(0)

        @pl.when(e == 0)
        def _():
            base = sc[1] * per_group + (sc[0] % 2) * local
            slot_row = lax.broadcasted_iota(jnp.int32, (CAP, tokens), 0).astype(F32)
            for side in range(2):
                table = t_refs[side][0]
                ids, slots, gates = (
                    table[:TOPK],
                    table[TOPK : 2 * TOPK] - CAP,
                    table[2 * TOPK : 3 * TOPK],
                )
                picks = []
                for k in range(local):
                    hit = ids == (base + k).astype(F32)
                    slot = jnp.sum(jnp.where(hit, slots, 0.0), axis=0, keepdims=True) + CAP
                    gate = jnp.sum(jnp.where(hit, gates, 0.0), axis=0, keepdims=True)
                    pick = slot_row == slot
                    weight = jnp.sum(jnp.where(pick, gate, 0.0), axis=1, keepdims=True)
                    gate_ref[k, side * CAP : (side + 1) * CAP, :] = jnp.broadcast_to(
                        weight, (CAP, LANES)
                    )
                    picks.append(jnp.where(pick, 1.0, 0.0))
                pick = jnp.concatenate(picks, axis=0)
                st_ref[side] = pick.T.astype(BF16)
                pick = pick.astype(BF16)
                for p in range(count):
                    cols = columns(sc, p, quarter)
                    block = jnp.concatenate(
                        [x_refs[2 * side][:, cols], x_refs[2 * side + 1][:, cols]], axis=0
                    )
                    got = dot_nn(pick, block).astype(BF16)
                    block = jnp.concatenate(
                        [g_refs[2 * side][0, :, cols], g_refs[2 * side + 1][0, :, cols]], axis=0
                    )
                    grad = dot_nn(pick, block)
                    for k in range(local):
                        rows = slice(side * CAP, (side + 1) * CAP)
                        d_ref[k, rows, p * quarter : (p + 1) * quarter] = got[
                            k * CAP : (k + 1) * CAP
                        ]
                        go_ref[k, rows, p * quarter : (p + 1) * quarter] = (
                            grad[k * CAP : (k + 1) * CAP] * gate_ref[k, rows, 0:1]
                        ).astype(BF16)

        gate = up = act_grad = None
        for p in range(count):
            cols = slice(p * quarter, (p + 1) * quarter)
            rows = d_ref[e, :, cols]
            a = dot_nn(rows, w_refs[p][0, 0])
            b = dot_nn(rows, w_refs[p][0, 1])
            c = dot_nn(go_ref[e, :, cols], w_refs[p][0, 2])
            gate = a if gate is None else gate + a
            up = b if up is None else up + b
            act_grad = c if act_grad is None else act_grad + c
        sig = jax.nn.sigmoid(gate)
        silu = gate * sig
        act = (silu * up).astype(BF16)
        up_grad = (act_grad * silu).astype(BF16)
        gate_grad = (act_grad * up * sig * (1.0 + gate * (1.0 - sig))).astype(BF16)
        h_ref[e, :, :hidden] = act
        h_ref[e, :, hidden : 2 * hidden] = gate_grad
        h_ref[e, :, 2 * hidden :] = up_grad
        weight = gate_ref[e, :, 0:1]
        for p in range(count):
            cols = slice(p * quarter, (p + 1) * quarter)
            ns_ref[e, :, cols] = (
                dot_nt(gate_grad, w_refs[p][0, 0]) + dot_nt(up_grad, w_refs[p][0, 1])
            ).astype(BF16)
            ys_ref[e, :, cols] = (dot_nt(act, w_refs[p][0, 2]) * weight).astype(BF16)

        @pl.when(e == local - 1)
        def _():
            for side, (n_ref, y_ref) in enumerate(((na_ref, ya_ref), (nb_ref, yb_ref))):
                place = st_ref[side]
                for p in range(count):
                    cols = slice(p * quarter, (p + 1) * quarter)
                    rows = slice(side * CAP, (side + 1) * CAP)
                    for source, target in ((ns_ref, n_ref), (ys_ref, y_ref)):
                        stacked = jnp.concatenate(
                            [source[k, rows, cols] for k in range(local)], axis=0
                        )
                        target[:, columns(sc, p, quarter)] = dot_nn(place, stacked).astype(
                            target.dtype
                        )

    group = lambda e, sc: (sc[1] ^ far, 0, 0)
    moved = 2 * count * local * 3 * quarter * hidden + 40 * tokens * model
    return pl.pallas_call(
        body,
        out_shape=[
            sds((tokens, model), F32),
            sds((tokens, model), BF16),
            sds((tokens, model), F32),
            sds((tokens, model), BF16),
            sds((local, 2 * CAP, model), BF16),
            sds((local, 2 * CAP, model), BF16),
            sds((local, 2 * CAP, 3 * hidden), BF16),
        ],
        grid_spec=pltpu.PrefetchScalarGridSpec(
            num_scalar_prefetch=1,
            grid=(local,),
            in_specs=[whole((half, model))] * 4
            + [pl.BlockSpec((1, half, model), group)] * 4
            + [pl.BlockSpec((1, 3 * TOPK, tokens), group)] * 2
            + [pl.BlockSpec((1, 3, quarter, hidden), lambda e, sc: (e, 0, 0, 0))] * count,
            out_specs=[whole((tokens, model))] * 4
            + [
                whole((local, 2 * CAP, model)),
                whole((local, 2 * CAP, model)),
                whole((local, 2 * CAP, 3 * hidden)),
            ],
            scratch_shapes=[
                pltpu.VMEM((2, tokens, side_rows), BF16),
                pltpu.VMEM((local, 2 * CAP, LANES), F32),
                pltpu.VMEM((local, 2 * CAP, model), BF16),
                pltpu.VMEM((local, 2 * CAP, model), BF16),
            ],
        ),
        compiler_params=params(),
        cost_estimate=cost(
            2 * local * 2 * CAP * model * (6 * hidden + 4 * tokens), moved, local * 2 * CAP * hidden
        ),
        name="experts",
    )(scalars, *rows_in, *grads_in, *tables, *weights)


def expert_weight_grads(row_sets, grad_sets, hidden_sets, quarter):
    groups = len(row_sets)
    local, rows, model = row_sets[0].shape
    hidden = hidden_sets[0].shape[2] // 3
    count = model // quarter
    step = min(groups, 4)

    def body(*refs):
        d_refs, go_refs, h_refs = refs[:groups], refs[groups : 2 * groups], refs[2 * groups : 3 * groups]
        out_refs = refs[3 * groups :]
        for p in range(count):
            cols = slice(p * quarter, (p + 1) * quarter)
            sums = [None, None, None]
            for start in range(0, groups, step):
                chosen = range(start, start + step)
                left = jnp.concatenate([d_refs[g][0, :, cols] for g in chosen], axis=0)
                left_out = jnp.concatenate([go_refs[g][0, :, cols] for g in chosen], axis=0)
                right = jnp.concatenate([h_refs[g][0] for g in chosen], axis=0)
                parts = (
                    dot_tn(left, right[:, hidden : 2 * hidden]),
                    dot_tn(left, right[:, 2 * hidden :]),
                    dot_tn(left_out, right[:, :hidden]),
                )
                sums = [a if b is None else a + b for a, b in zip(parts, sums)]
            for k in range(3):
                out_refs[p][0, k] = sums[k].astype(out_refs[p].dtype)

    by_expert = lambda shape: pl.BlockSpec((1,) + shape, lambda e: (e,) + (0,) * len(shape))
    out = (local, 3, quarter, hidden)
    return pl.pallas_call(
        body,
        out_shape=[sds(out, F32), sds(out, F32), sds(out, BF16), sds(out, BF16)],
        grid=(local,),
        in_specs=[by_expert((rows, model))] * (2 * groups)
        + [by_expert((rows, 3 * hidden))] * groups,
        out_specs=[by_expert((3, quarter, hidden))] * 4,
        compiler_params=params(),
        cost_estimate=cost(
            6 * local * rows * groups * model * hidden,
            2 * groups * local * rows * (2 * model + 3 * hidden) + 3 * local * 3 * model * hidden,
        ),
        name="expert_weight_grads",
    )(*row_sets, *grad_sets, *hidden_sets)


def middle_grad(scalars, parts, residual, grad_out, gains):
    tokens, model = grad_out.shape
    half = tokens // 2
    count = len(parts)

    def body(sc, *refs):
        part_refs = refs[:count]
        res_ref, go_ref, gain_ref, rg_ref, branch_ref, sum_ref = refs[count:]
        total = part_refs[0][...].astype(F32)
        for k in range(1, count):
            total = total + part_refs[k][...].astype(F32)
        residual = res_ref[...]
        start = pl.multiple_of(sc[2] * half, half)
        inverse = lax.rsqrt(jnp.mean(residual * residual, axis=-1, keepdims=True) + EPS)
        scaled = gain_ref[1:2, :] * total
        shift = jnp.mean(scaled * residual, axis=-1, keepdims=True)
        grad = (
            go_ref[pl.ds(start, half)].astype(F32)
            + inverse * scaled
            - residual * (inverse * inverse * inverse * shift)
        )
        rg_ref[...] = grad
        branch_ref[...] = grad.astype(BF16)
        sum_ref[...] = jnp.broadcast_to(
            jnp.sum(total * residual * inverse, axis=0, keepdims=True), (8, model)
        )

    return pl.pallas_call(
        body,
        out_shape=[sds((half, model), F32), sds((half, model), BF16), sds((8, model), F32)],
        grid_spec=pltpu.PrefetchScalarGridSpec(
            num_scalar_prefetch=1,
            grid=(1,),
            in_specs=[whole((half, model))] * (count + 1)
            + [whole((tokens, model)), whole((8, model))],
            out_specs=[whole((half, model)), whole((half, model)), whole((8, model))],
        ),
        compiler_params=params(),
        cost_estimate=cost(20 * half * model, 24 * half * model),
        name="middle_grad",
    )(scalars, *parts, residual, grad_out, gains)


def attend_grad(scalars, branch, queries, kv_all, lse, out_pieces, cos_table, sin_table, piece_count):
    tokens, q_width = queries.shape
    length, kv2 = kv_all.shape
    kv_width = kv2 // 2
    kv_heads = kv_width // HEAD_DIM
    pair_blocks = kv_width // LANES
    count = len(out_pieces)
    quarter = out_pieces[0].shape[0]
    model = quarter * count
    half = tokens // 2

    def body(sc, b0_ref, b1_ref, q_ref, k_ref, v_ref, lse_ref, cos_ref, sin_ref, *rest):
        out_refs = rest[:count]
        dq_ref, dkv_ref, mg_ref, bias_ref = rest[count:]
        c = pl.program_id(0)

        @pl.when(c == 0)
        def _():
            cols = lax.broadcasted_iota(jnp.int32, (length, tokens), 0)
            rows = lax.broadcasted_iota(jnp.int32, (length, tokens), 1)
            query_pos = token_position(sc, rows, sc[1], tokens)
            key_pos = token_position(sc, cols % tokens, cols // tokens, tokens)
            bias_ref[...] = seen_bias(sc, query_pos, key_pos, piece_count)
            total = None
            for p in range(count):
                col = columns(sc, p, quarter)
                block = jnp.concatenate([b0_ref[:, col], b1_ref[:, col]], axis=0)
                part = dot_nn(block, out_refs[p][...])
                total = part if total is None else total + part
            mg_ref[...] = total.astype(BF16)

        low = lax.broadcasted_iota(jnp.int32, (1, LANES), 1) < HEAD_DIM
        mine = low == (c % 2 == 0)
        keys = k_ref[...].astype(F32)
        keys = jnp.where(mine, keys, pltpu.roll(keys, HEAD_DIM, 1)).astype(BF16)
        vals = v_ref[...].astype(F32)
        vals = jnp.where(mine, vals, pltpu.roll(vals, HEAD_DIM, 1)).astype(BF16)
        query = q_ref[...]
        grad = mg_ref[:, pl.ds(pl.multiple_of(c * LANES, LANES), LANES)]
        zero = jnp.zeros_like(query)
        lse_t = lse_ref[...].T
        dqs = []
        dk = dv = None
        for g in range(2):
            query_g = jnp.where(low, query, zero) if g == 0 else jnp.where(low, zero, query)
            grad_g = jnp.where(low, grad, zero) if g == 0 else jnp.where(low, zero, grad)
            scores = dot_nt(keys, query_g) + bias_ref[...]
            probs = jnp.exp(scores - lse_t[g * HEAD_DIM : g * HEAD_DIM + 1])
            prob_grad = dot_nt(vals, grad_g)
            delta = jnp.sum(probs * prob_grad, axis=0, keepdims=True)
            score_grad = (probs * (prob_grad - delta)).astype(BF16)
            dqs.append(dot_tn(score_grad, keys))
            dk_g = dot_nn(score_grad, query_g)
            dv_g = dot_nn(probs.astype(BF16), grad_g)
            dk = dk_g if dk is None else dk + dk_g
            dv = dv_g if dv is None else dv + dv_g
        dq = jnp.where(low, dqs[0], dqs[1]) * HEAD_DIM**-0.5
        dq_ref[...] = turn(dq, cos_ref[...], -sin_ref[...]).astype(BF16)
        for k, value in ((0, dk), (pair_blocks, dv)):
            value = (value + pltpu.roll(value, HEAD_DIM, 1)).astype(BF16)
            where = pl.ds(pl.multiple_of((k + c // 2) * LANES, LANES), LANES)
            dkv_ref[:, where] = jnp.where(mine, value, dkv_ref[:, where])

    return pl.pallas_call(
        body,
        out_shape=[sds((tokens, q_width), BF16), sds((length, kv2), BF16)],
        grid_spec=pltpu.PrefetchScalarGridSpec(
            num_scalar_prefetch=1,
            grid=(kv_heads,),
            in_specs=[
                whole((half, model)),
                whole((half, model)),
                pl.BlockSpec((tokens, LANES), lambda c, sc: (0, c)),
                pl.BlockSpec((length, LANES), lambda c, sc: (0, c // 2)),
                pl.BlockSpec((length, LANES), lambda c, sc: (0, pair_blocks + c // 2)),
                pl.BlockSpec((tokens, LANES), lambda c, sc: (0, c)),
                whole((tokens, LANES)),
                whole((tokens, LANES)),
            ]
            + [whole(p.shape) for p in out_pieces],
            out_specs=[
                pl.BlockSpec((tokens, LANES), lambda c, sc: (0, c)),
                whole((length, kv2)),
            ],
            scratch_shapes=[
                pltpu.VMEM((tokens, q_width), BF16),
                pltpu.VMEM((length, tokens), F32),
            ],
        ),
        compiler_params=params(),
        cost_estimate=cost(
            40 * tokens * length * LANES + 2 * tokens * q_width * model,
            6 * length * kv2 + 8 * tokens * model,
            2 * kv_heads * tokens * length,
        ),
        name="attend_grad",
    )(scalars, *branch, queries, kv_all, kv_all, lse, cos_table, sin_table, *out_pieces)


def outer(scalars, left, right, extra, quarter, name):
    tokens, model = right.shape[0], left[0].shape[1]
    width = right.shape[1]
    count = model // quarter
    out_width = width + (LANES if extra is not None else 0)
    extras = [] if extra is None else [extra]

    def body(sc, *refs):
        left_refs, refs = refs[: len(left)], refs[len(left) :]
        right_ref, refs = refs[0], refs[1:]
        extra_refs, out_refs = refs[: len(extras)], refs[len(extras) :]
        values = right_ref[...]
        for p in range(count):
            cols = columns(sc, p, quarter)
            blocks = [r[:, cols] for r in left_refs]
            block = blocks[0] if len(blocks) == 1 else jnp.concatenate(blocks, axis=0)
            out_refs[p][:, :width] = dot_tn(block, values).astype(out_refs[p].dtype)
            if extras:
                rows = lax.broadcasted_iota(jnp.int32, (quarter, quarter), 0)
                diagonal = rows == lax.broadcasted_iota(jnp.int32, (quarter, quarter), 1)
                row = extra_refs[0][0:1, cols]
                column = jnp.sum(jnp.where(diagonal, row, 0.0), axis=1, keepdims=True)
                out_refs[p][:, width:] = jnp.broadcast_to(column, (quarter, LANES)).astype(
                    out_refs[p].dtype
                )

    out = (quarter, out_width)
    return pl.pallas_call(
        body,
        out_shape=[sds(out, F32), sds(out, BF16), sds(out, F32), sds(out, BF16)],
        grid_spec=pltpu.PrefetchScalarGridSpec(
            num_scalar_prefetch=1,
            grid=(1,),
            in_specs=[whole(a.shape) for a in (*left, right, *extras)],
            out_specs=[whole(out)] * 4,
        ),
        compiler_params=params(),
        cost_estimate=cost(
            2 * tokens * model * width, 2 * tokens * (model + width) + 3 * model * width
        ),
        name=name,
    )(scalars, *left, right, *extras)


def reduce_rows(parts):
    own, send, far, far_send = parts
    kept = own + swap(send, "shard", 1).astype(F32)
    passed = (far + swap(far_send, "shard", 1).astype(F32)).astype(BF16)
    total = (kept + swap(passed, "shard", 2).astype(F32)).astype(BF16)
    groups = lax.axis_size("ctx")
    rows = total.shape[0] // groups
    got = lax.all_to_all(total.reshape(groups, rows, total.shape[1]), "ctx", 0, 0, tiled=True)
    return jnp.sum(got.astype(F32), axis=0)


def back(scalars, dq, dkv, normed, pieces, cos_table, sin_table):
    tokens, model = normed.shape
    groups, _, kv2 = dkv.shape
    q_width = dq.shape[1]
    kv_width = kv2 // 2
    heads = q_width + kv2
    count = len(pieces)
    quarter = pieces[0].shape[0]
    half = tokens // 2

    def body(sc, dq_ref, dkv_ref, xn_ref, cos_ref, sin_ref, *rest):
        piece_refs = rest[:count]
        own_ref, send_ref = rest[count : count + 2]
        grad_refs = rest[count + 2 :]
        total = dkv_ref[0].astype(F32)
        for g in range(1, groups):
            total = total + dkv_ref[g].astype(F32)
        dk = turn(total[:, :kv_width], cos_ref[...], -sin_ref[...]).astype(BF16)
        dl_kv = jnp.concatenate([dk, total[:, kv_width:].astype(BF16)], axis=1)
        dl_q = dq_ref[...]
        for p in range(count):
            cols = columns(sc, p, quarter)
            part = dot_nt(dl_q, piece_refs[p][:, :q_width]) + dot_nt(
                dl_kv, piece_refs[p][:, q_width:heads]
            )
            own_ref[:, cols] = part[:half]
            send_ref[:, cols] = part[half:].astype(BF16)
            grad_refs[p][...] = dot_tn(xn_ref[:, cols], dl_kv).astype(grad_refs[p].dtype)

    out = (quarter, kv2)
    return pl.pallas_call(
        body,
        out_shape=[
            sds((half, model), F32),
            sds((half, model), BF16),
            sds(out, F32),
            sds(out, BF16),
            sds(out, F32),
            sds(out, BF16),
        ],
        grid_spec=pltpu.PrefetchScalarGridSpec(
            num_scalar_prefetch=1,
            grid=(1,),
            in_specs=[
                whole(a.shape) for a in (dq, dkv, normed, cos_table, sin_table, *pieces)
            ],
            out_specs=[whole((half, model))] * 2 + [whole(out)] * 4,
        ),
        compiler_params=params(),
        cost_estimate=cost(
            2 * tokens * model * (heads + kv2), 2 * model * (heads + 4 * tokens + 2 * kv2)
        ),
        name="back",
    )(scalars, dq, dkv, normed, cos_table, sin_table, *pieces)


def last_grad(scalars, layer_input, own, received, residual_grad, gains):
    tokens, model = layer_input.shape
    half = tokens // 2

    def body(sc, x_ref, own_ref, rec_ref, rg_ref, gain_ref, out_ref):
        start = pl.multiple_of(sc[2] * half, half)
        values = x_ref[pl.ds(start, half)].astype(F32)
        inverse = lax.rsqrt(jnp.mean(values * values, axis=-1, keepdims=True) + EPS)
        scaled = gain_ref[0:1, :] * (own_ref[...] + rec_ref[...].astype(F32))
        shift = jnp.mean(scaled * values, axis=-1, keepdims=True)
        out_ref[...] = (
            rg_ref[...] + inverse * scaled - values * (inverse * inverse * inverse * shift)
        ).astype(BF16)

    return pl.pallas_call(
        body,
        out_shape=sds((half, model), BF16),
        grid_spec=pltpu.PrefetchScalarGridSpec(
            num_scalar_prefetch=1,
            grid=(1,),
            in_specs=[
                whole((tokens, model)),
                whole((half, model)),
                whole((half, model)),
                whole((half, model)),
                whole((8, model)),
            ],
            out_specs=whole((half, model)),
        ),
        compiler_params=params(),
        cost_estimate=cost(12 * half * model, 14 * half * model),
        name="last_grad",
    )(scalars, layer_input, own, received, residual_grad, gains)


def local(
    layer_input,
    attn_norm,
    w_query,
    w_key,
    w_value,
    w_out,
    moe_norm,
    expert_weights,
    expert_ids,
    slot_ids,
    gate_values,
    piece_starts,
    grad_out,
):
    _, tokens, model = layer_input.shape
    half = tokens // 2
    groups = lax.axis_size("ctx")
    shard = lax.axis_index("shard")
    group = lax.axis_index("ctx")
    side = lax.axis_index("tp")
    piece_count = piece_starts.shape[1]
    scalars = jnp.concatenate(
        [jnp.stack([shard, group, side]).astype(jnp.int32), piece_starts[0]]
    )
    flat_input = layer_input[0]
    flat_grad = grad_out[0]
    q_width, kv_width = w_query.shape[1], w_key.shape[1]
    rows_here = w_query.shape[0]
    quarter = rows_here * groups

    qkv_block = jnp.concatenate(
        [
            w_query,
            w_key,
            w_value,
            attn_norm[:, None],
            moe_norm[:, None],
            jnp.zeros((rows_here, LANES - 2), BF16),
        ],
        axis=1,
    )
    block_0 = spread(qkv_block, "ctx").reshape(quarter, -1)
    block_2 = swap(block_0, "shard", 2)
    qkv_pieces = [block_0, swap(block_0, "shard", 1), block_2, swap(block_2, "shard", 1)]

    out_0 = spread(w_out.T, "ctx").reshape(quarter, -1)
    out_0, block_2 = lax.optimization_barrier((out_0, block_2))
    out_2 = swap(out_0, "shard", 2)
    out_pieces = [out_0, swap(out_0, "shard", 1), out_2, swap(out_2, "shard", 1)]

    table = jnp.concatenate(
        [
            expert_ids[0].T.astype(F32),
            slot_ids[0].T.astype(F32),
            gate_values[0].T,
        ],
        axis=0,
    )
    table = jnp.where(
        side == 0, table, jnp.concatenate([table[:, half:], table[:, :half]], axis=1)
    )
    table_own = spread(table, "ctx")
    table_mate = swap(table_own, "shard", 1)

    local_experts = expert_weights.shape[0] // 2
    core = shard % 2
    mine = lax.dynamic_slice_in_dim(expert_weights, core * local_experts, local_experts, 0)
    given = lax.dynamic_slice_in_dim(expert_weights, (1 - core) * local_experts, local_experts, 0)
    taken = swap(given, "shard", 1)
    mine, taken, out_2 = lax.optimization_barrier((mine, taken, out_2))
    expert_pieces = [mine, taken, swap(mine, "shard", 2), swap(taken, "shard", 2)]

    positions = (
        group * tokens + (jnp.arange(tokens, dtype=jnp.int32) ^ (side * half).astype(jnp.int32))
    ).astype(F32)
    lane = jnp.arange(LANES, dtype=jnp.int32)
    step = (lane % (HEAD_DIM // 2)).astype(F32)
    angles = positions[:, None] * (1.0 / 10000.0 ** (step * 2.0 / HEAD_DIM))[None, :]
    cos_table = jnp.cos(angles)
    sin_table = jnp.sin(angles) * jnp.where(lane % HEAD_DIM < HEAD_DIM // 2, -1.0, 1.0)[None, :]

    normed_one, queries, kv_here, gains = front(
        scalars, flat_input, qkv_pieces, cos_table, sin_table, (q_width, kv_width)
    )
    kv_all = spread(kv_here, "ctx").reshape(groups * tokens, 2 * kv_width)

    own_grad = lax.dynamic_slice_in_dim(flat_grad, side * half, half, 0)
    own_grad, kv_all = lax.optimization_barrier((own_grad, kv_all))
    grads_a0 = spread(own_grad, "ctx")
    grads_a1 = swap(grads_a0, "tp", 1)
    grads_in = [grads_a0, grads_a1, swap(grads_a0, "shard", 1), swap(grads_a1, "shard", 1)]

    mixed, lse, attention_own, attention_send = attend(
        scalars, queries, kv_all, out_pieces, piece_count
    )
    residual, normed_two = second_norm(
        scalars, flat_input, attention_own, swap(attention_send, "tp", 1), gains
    )

    norm_parts, out_parts = [], []
    row_sets, grad_sets, hidden_sets = [], [], []
    arrived = [normed_two] + [swap(normed_two, "ctx", b) for b in range(1, groups)]
    for b in range(groups):
        a0 = arrived[b]
        a1 = swap(a0, "tp", 1)
        rows_in = [a0, a1, swap(a0, "shard", 1), swap(a1, "shard", 1)]
        norm_a, norm_b, out_a, out_b, rows, grads, hiddens = experts(
            scalars, b, rows_in, grads_in, [table_own, table_mate], expert_pieces, None
        )
        row_sets.append(rows)
        grad_sets.append(grads)
        hidden_sets.append(hiddens)
        for parts, own, mate in ((norm_parts, norm_a, norm_b), (out_parts, out_a, out_b)):
            both = swap(mate, "shard", 1)
            sent = (own[half:] + both[half:].astype(F32)).astype(BF16)
            kept = own[:half] + both[:half].astype(F32) + swap(sent, "tp", 1).astype(F32)
            parts.append(kept if b == 0 else swap(kept.astype(BF16), "ctx", b))

    residual_grad, branch_own, gain_row = middle_grad(
        scalars, norm_parts, residual, flat_grad, gains
    )
    branch = [branch_own, swap(branch_own, "tp", 1)]

    def natural(own):
        other = swap(own, "tp", 1)
        return jnp.where(
            side == 0,
            jnp.concatenate([own, other], axis=0),
            jnp.concatenate([other, own], axis=0),
        )[None]

    out_sum = residual
    for part in out_parts:
        out_sum = out_sum + part.astype(F32)
    output = natural(out_sum.astype(BF16))

    keep_0, keep_1, send_2, send_3 = expert_weight_grads(
        row_sets, grad_sets, hidden_sets, expert_pieces[0].shape[2]
    )
    grad_0 = keep_0 + swap(send_2, "shard", 2).astype(F32)
    grad_1 = (keep_1 + swap(send_3, "shard", 2).astype(F32)).astype(BF16)
    grad_1 = swap(grad_1, "shard", 1).astype(F32)
    expert_grad = jnp.where(
        core == 0,
        jnp.concatenate([grad_0, grad_1], axis=0),
        jnp.concatenate([grad_1, grad_0], axis=0),
    )

    out_grad = reduce_rows(outer(scalars, branch, mixed, gain_row, quarter, "out_grad"))
    moe_sum = out_grad[:, q_width]
    moe_norm_grad = moe_sum + swap(moe_sum, "tp", 1)
    out_grad = out_grad[:, :q_width].T

    dq, dkv_parts = attend_grad(
        scalars, branch, queries, kv_all, lse, out_pieces, cos_table, sin_table, piece_count
    )
    dkv = lax.all_to_all(
        dkv_parts.reshape(groups, tokens, 2 * kv_width), "ctx", 0, 0, tiled=True
    )
    query_grad = reduce_rows(outer(scalars, [normed_one], dq, None, quarter, "query_grad"))
    normed_own, normed_send, *kv_parts = back(
        scalars, dq, dkv, normed_one, qkv_pieces, cos_table, sin_table
    )
    input_half = last_grad(
        scalars, flat_input, normed_own, swap(normed_send, "tp", 1), residual_grad, gains
    )
    input_grad = natural(input_half)
    kv_grad = reduce_rows(kv_parts)
    key_grad, value_grad = kv_grad[:, :kv_width], kv_grad[:, kv_width:]
    attn_sum = (
        jnp.sum(w_query.astype(F32) * query_grad, axis=1)
        + jnp.sum(w_key.astype(F32) * key_grad, axis=1)
        + jnp.sum(w_value.astype(F32) * value_grad, axis=1)
    )
    attn_norm_grad = (attn_sum + swap(attn_sum, "tp", 1)) / attn_norm.astype(F32)
    return (
        output,
        input_grad,
        attn_norm_grad,
        query_grad,
        key_grad,
        value_grad,
        out_grad,
        moe_norm_grad,
        expert_grad,
    )


def solution(mesh):
    in_specs = (
        P("shard", "ctx", None),
        P(("shard", "ctx")),
        P(("shard", "ctx"), "tp"),
        P(("shard", "ctx"), "tp"),
        P(("shard", "ctx"), "tp"),
        P("tp", ("shard", "ctx")),
        P(("shard", "ctx")),
        P("ctx", None, "shard", "tp"),
        P("shard", "ctx", None),
        P("shard", "ctx", None),
        P("shard", "ctx", None),
        P("shard", None),
        P("shard", "ctx", None),
    )
    out_specs = (
        P("shard", "ctx", None),
        P("shard", "ctx", None),
        P(("shard", "ctx")),
        P(("shard", "ctx"), "tp"),
        P(("shard", "ctx"), "tp"),
        P(("shard", "ctx"), "tp"),
        P("tp", ("shard", "ctx")),
        P(("shard", "ctx")),
        P("ctx", None, "shard", "tp"),
    )
    return jax.shard_map(local, mesh=mesh, in_specs=in_specs, out_specs=out_specs, check_vma=False)
```

time: 1710 us -> 470 us (0.27)
  waiting for transfers between devices: 1160 us -> 173 us
  local copies, waits for them, and re-layouts: 149 us -> 16.6 us
  matrix products: 120 us -> 0 us
  Pallas kernels: 0 us -> 115 us
  blocking collectives: 170 us -> 60.4 us
  starting transfers between devices: 25.1 us -> 65.6 us
  other arithmetic: 56.2 us -> 36 us
    all_to_all x4 -> x6, waiting for transfers between devices: 740 us -> 35.8 us  [the longest x2 29.8 us: spread(): return lax.all_to_all(copies, axis, 0, 0, tiled=True)]
    reduce_scatter x7 -> x0, waiting for transfers between devices: 319 us -> none  [the longest x1 64.9 us: local(): lax.psum_scatter(query_w_grad, ('shard', 'ctx'), scatter_dimension=0, til...]
    ppermute x0 -> x69, waiting for transfers between devices: none -> 137 us  [swap(): return lax.ppermute(value, axis, [(i, i ^ distance) for i in range(size)])]
    dot_general x39 -> x0, matrix products: 120 us -> none  [the longest x6 15 us: block_scores(): jnp.einsum('sqhgd,skhd->shgqk', queries, key_block, preferred_element_typ...]
    pallas_call x0 -> x14, Pallas kernels: none -> 115 us  [the longest x4 53.4 us: experts(): pl.pallas_call(body, out_shape=[sds((tokens, model), F32), sds((tokens, m...]
    all_gather x4 -> x0, blocking collectives: 99.4 us -> none  [the longest x1 34.8 us: local(): lax.all_gather(w_value, ('shard', 'ctx'), axis=0, tiled=True)]
    psum x3 -> x0, waiting for transfers between devices: 97.1 us -> none  [the longest x1 61.1 us: local(): moe_sum, normed_two_grad = lax.psum((moe_part, normed_part), 'tp')]
    unnamed x2 -> x0, blocking collectives: 70.1 us -> none
  transfers between devices with their start and end apart: 17 -> 75, of which waited for: 14 -> 18; matrix products, arithmetic and copies ran while one was open for 12% -> 8% of each run, Pallas kernels for 0% -> 23%
where the time goes in v1:
time: 470 us; the launch traced here: 468 us
  waiting for transfers between devices  173 us (37%)
  Pallas kernels  115 us (24%)
  starting transfers between devices  65.6 us (14%)
  blocking collectives  60.4 us (13%)
  other arithmetic  36 us (8%)
  local copies, waits for them, and re-layouts  16.6 us (4%)
    ppermute x69, waiting for transfers between devices, swap(): return lax.ppermute(value, axis, [(i, i ^ distance) for i in range(size)])  137 us
    all_to_all x3, blocking collectives, spread(): return lax.all_to_all(copies, axis, 0, 0, tiled=True)  60.4 us
    pallas_call x4, Pallas kernels, experts(): pl.pallas_call(body, out_shape=[sds((tokens, model), F32), sds((tokens, m...  53.4 us
    ppermute x69, starting transfers between devices, swap(): return lax.ppermute(value, axis, [(i, i ^ distance) for i in range(size)])  38.7 us
    all_to_all x2, waiting for transfers between devices, spread(): return lax.all_to_all(copies, axis, 0, 0, tiled=True)  29.8 us
    all_to_all x3, starting transfers between devices, reduce_rows(): lax.all_to_all(total.reshape(groups, rows, total.shape[1]), 'ctx', 0, 0,...  14.7 us
    pallas_call x1, Pallas kernels, attend_grad(): pl.pallas_call(body, out_shape=[sds((tokens, q_width), BF16), sds((length...  13.5 us
    pallas_call x1, Pallas kernels, expert_weight_grads(): pl.pallas_call(body, out_shape=[sds(out, F32), sds(out, F32), sds(out, BF...  11.4 us
  transfers between devices with their start and end apart: 75, of which 18 were waited for; matrix products, arithmetic and copies ran while one was open for 8% of the time, Pallas kernels for 23%

profile of v1, /device:TPU:0, one launch (start us, length us, event | category | flops | bytes accessed | tf_op | source)
XLA Modules:
  0.0 468.3 jit_solution(2236645041103363125)
XLA Ops:
  3.2 22.0 %all_to_all.45 = bf16[4,64,1152]{2,1,0:T(8,128)(2,1)S(1)} all-to-all(bf16[4,64,1152]{2,1,0:T(8,128)(2,1)S(1)} %broadcast_in_dim.25), channel_id=1, replica_groups=mesh['shard'=4,'ctx'=4,'tp'=2] {'ctx'}, dimensions={0} | all-to-all | bytes 1179648 | tf_op jit(solution)/shard_map/all_to_all | solution.py:30
  26.7 12.7 %collective-permute-done.1.rest_2_ = bf16[256,1152]{1,0:T(8,128)(2,1)S(1)} collective-permute-done((bf16[256,1152]{1,0:T(8,128)(2,1)S(1)}, bf16[256,1152]{1,0:T(8,128)(2,1)S(1)}, u32[]{:S(2)}, u32[]{:S(2)}) %collective-permute-start.1) | collective-permute-done | bytes 589856 | tf_op jit(solution)/shard_map/ppermute | solution.py:24
  48.8 30.0 %all_to_all.46 = bf16[4,256,512]{2,1,0:T(8,128)(2,1)} all-to-all(bf16[4,256,512]{2,1,0:T(8,128)(2,1)S(1)} %broadcast_in_dim.27), channel_id=1, replica_groups=mesh['shard'=4,'ctx'=4,'tp'=2] {'ctx'}, dimensions={0} | all-to-all | bytes 2097152 | tf_op jit(solution)/shard_map/all_to_all | solution.py:30
  83.6 8.8 %all-to-all-done.2 = bf16[4,64,512]{2,1,0:T(8,128)(2,1)} async-done(((bf16[4,64,512]{2,1,0:T(8,128)(2,1)}), bf16[4,64,512]{2,1,0:T(8,128)(2,1)}, u32[]{:S(2)}, u32[]{:S(2)}) %all-to-all-start.2) | async-done | bytes 262176 | tf_op jit(solution)/shard_map/all_to_all | solution.py:30
  101.2 21.0 %all-to-all-done.3.refs_4_ = bf16[4,128,1024]{2,1,0:T(8,128)(2,1)} async-done(((bf16[4,128,1024]{2,1,0:T(8,128)(2,1)}), bf16[4,128,1024]{2,1,0:T(8,128)(2,1)}, u32[]{:S(2)}, u32[]{:S(2)}) %all-to-all-start.3) | async-done | bytes 1048608 | tf_op jit(solution)/shard_map/all_to_all | solution.py:30
  128.7 10.1 %attend.1 = (bf16[256,512]{1,0:T(8,128)(2,1)}, f32[256,512]{1,0:T(8,128)}, f32[128,1024]{1,0:T(8,128)}, bf16[128,1024]{1,0:T(8,128)(2,1)}) custom-call(s32[4]{0:T(128)} %pad_add_fusion.sc, bf16[256,512]{1,0:T(8,128)(2,1)} %get-tuple-element.75.q_ref, bf16[1024,512]{1,0:T(8,128)(2,1)} %bitcast.45, bf16[1024,512]{1,0:T(8,128)(2,1)} %bitcast.46, ...), custom_call_target="tpu_custom_call" | custom-call | flops 805306368 | bytes 4194304 | tf_op jit(solution)/shard_map/attend/pallas_call | solution.py:223
  139.4 9.2 %collective-permute-done.10.refs_5_ = bf16[4,128,1024]{2,1,0:T(8,128)(2,1)} collective-permute-done((bf16[4,128,1024]{2,1,0:T(8,128)(2,1)}, bf16[4,128,1024]{2,1,0:T(8,128)(2,1)}, u32[]{:S(2)}, u32[]{:S(2)}) %collective-permute-start.10) | collective-permute-done | bytes 1048608 | tf_op jit(solution)/shard_map/ppermute | solution.py:24
  148.7 8.4 %all_to_all.47.refs_8_ = f32[4,24,256]{2,1,0:T(8,128)S(1)} all-to-all(f32[4,24,256]{2,1,0:T(8,128)S(1)} %broadcast_in_dim.30), channel_id=1, replica_groups=mesh['shard'=4,'ctx'=4,'tp'=2] {'ctx'}, dimensions={0} | all-to-all | bytes 196608 | tf_op jit(solution)/shard_map/all_to_all | solution.py:30
  163.4 29.5 %collective-permute-done.16.refs_13_ = bf16[4,3,256,256]{3,2,1,0:T(8,128)(2,1)} collective-permute-done((bf16[4,3,256,256]{3,2,1,0:T(8,128)(2,1)S(1)}, bf16[4,3,256,256]{3,2,1,0:T(8,128)(2,1)}, u32[]{:S(2)}, u32[]{:S(2)}) %collective-permute-start.16) | collective-permute-done | bytes 1572896 | tf_op jit(solution)/shard_map/ppermute | solution.py:24
  193.5 6.0 %collective-permute-done.19.refs_0_ = bf16[128,1024]{1,0:T(8,128)(2,1)S(1)} collective-permute-done((bf16[128,1024]{1,0:T(8,128)(2,1)}, bf16[128,1024]{1,0:T(8,128)(2,1)S(1)}, u32[]{:S(2)}, u32[]{:S(2)}) %collective-permute-start.19) | collective-permute-done | bytes 262176 | tf_op jit(solution)/shard_map/ppermute | solution.py:24
  200.5 6.3 %collective-permute-done.27.refs_1_ = bf16[128,1024]{1,0:T(8,128)(2,1)S(1)} collective-permute-done((bf16[128,1024]{1,0:T(8,128)(2,1)S(1)}, bf16[128,1024]{1,0:T(8,128)(2,1)S(1)}, u32[]{:S(2)}, u32[]{:S(2)}) %collective-permute-start.27) | collective-permute-done | bytes 262176 | tf_op jit(solution)/shard_map/ppermute | solution.py:24
  210.0 13.3 %experts.7 = (f32[256,1024]{1,0:T(8,128)}, bf16[256,1024]{1,0:T(8,128)(2,1)}, f32[256,1024]{1,0:T(8,128)}, bf16[256,1024]{1,0:T(8,128)(2,1)}, bf16[4,192,1024]{2...) custom-call(s32[4]{0:T(128)} %pad_add_fusion.sc, bf16[128,1024]{1,0:T(8,128)(2,1)} %copy-done.54, ...), custom_call_target="tpu_custom_call" | custom-call | flops 4026531840 | bytes 16777216 | tf_op jit(solution)/shard_map/experts/pallas_call | solution.py:395
  224.7 13.3 %experts.6 = (f32[256,1024]{1,0:T(8,128)}, bf16[256,1024]{1,0:T(8,128)(2,1)}, f32[256,1024]{1,0:T(8,128)}, bf16[256,1024]{1,0:T(8,128)(2,1)}, bf16[4,192,1024]{2...) custom-call(s32[4]{0:T(128)} %pad_add_fusion.sc, bf16[128,1024]{1,0:T(8,128)(2,1)} %copy-done.50, ...), custom_call_target="tpu_custom_call" | custom-call | flops 4026531840 | bytes 16777216 | tf_op jit(solution)/shard_map/experts/pallas_call | solution.py:395
  239.2 13.2 %experts.5 = (f32[256,1024]{1,0:T(8,128)}, bf16[256,1024]{1,0:T(8,128)(2,1)}, f32[256,1024]{1,0:T(8,128)}, bf16[256,1024]{1,0:T(8,128)(2,1)}, bf16[4,192,1024]{2...) custom-call(s32[4]{0:T(128)} %pad_add_fusion.sc, bf16[128,1024]{1,0:T(8,128)(2,1)} %copy-done.48, ...), custom_call_target="tpu_custom_call" | custom-call | flops 4026531840 | bytes 16777216 | tf_op jit(solution)/shard_map/experts/pallas_call | solution.py:395
  253.4 13.5 %experts.4 = (f32[256,1024]{1,0:T(8,128)}, bf16[256,1024]{1,0:T(8,128)(2,1)}, f32[256,1024]{1,0:T(8,128)}, bf16[256,1024]{1,0:T(8,128)(2,1)}, bf16[4,192,1024]{2...) custom-call(s32[4]{0:T(128)} %pad_add_fusion.sc, ...), custom_call_target="tpu_custom_call" | custom-call | flops 4026531840 | bytes 16777216 | tf_op jit(solution)/shard_map/experts/pallas_call | solution.py:395
  267.0 11.4 %expert_weight_grads.1 = (f32[4,3,256,256]{3,2,1,0:T(8,128)}, f32[4,3,256,256]{3,2,1,0:T(8,128)}, bf16[4,3,256,256]{3,2,1,0:T(8,128)(2,1)}, bf16[4,3,256,256]{3,2,1,0:T(8,128)(2,1)}) custom-call(bf16[4,192,1024]{2,1,0:T(8,128)(2,1)} %get-tuple-element.125.refs_0_, bf16[4,192,1024]{2,1,0:T(8,128)(2,1)} %get-tuple-element.126.refs_1_, ...), custom_call_target="tpu_custom_call" | custom-call | flops 4831838208 | bytes 26738688 | tf_op jit(solution)/shard_map/expert_weight_grads/pallas_call | solution.py:463
  287.1 8.2 %collective-permute-done.50 = bf16[128,1024]{1,0:T(8,128)(2,1)S(1)} collective-permute-done((bf16[128,1024]{1,0:T(8,128)(2,1)S(1)}, bf16[128,1024]{1,0:T(8,128)(2,1)S(1)}, u32[]{:S(2)}, u32[]{:S(2)}) %collective-permute-start.50) | collective-permute-done | bytes 262176 | tf_op jit(solution)/shard_map/ppermute | solution.py:24
  296.0 10.5 %collective-permute-done.47 = bf16[128,1024]{1,0:T(8,128)(2,1)S(1)} collective-permute-done((bf16[128,1024]{1,0:T(8,128)(2,1)S(1)}, bf16[128,1024]{1,0:T(8,128)(2,1)S(1)}, u32[]{:S(2)}, u32[]{:S(2)}) %collective-permute-start.47) | collective-permute-done | bytes 262176 | tf_op jit(solution)/shard_map/ppermute | solution.py:24
  306.7 5.5 %collective-permute-done.44 = bf16[128,1024]{1,0:T(8,128)(2,1)S(1)} collective-permute-done((bf16[128,1024]{1,0:T(8,128)(2,1)S(1)}, bf16[128,1024]{1,0:T(8,128)(2,1)S(1)}, u32[]{:S(2)}, u32[]{:S(2)}) %collective-permute-start.44) | collective-permute-done | bytes 262176 | tf_op jit(solution)/shard_map/ppermute | solution.py:24
  320.5 10.5 %collective-permute-done.48.refs_2_ = bf16[128,1024]{1,0:T(8,128)(2,1)S(1)} collective-permute-done((bf16[128,1024]{1,0:T(8,128)(2,1)S(1)}, bf16[128,1024]{1,0:T(8,128)(2,1)S(1)}, u32[]{:S(2)}, u32[]{:S(2)}) %collective-permute-start.48) | collective-permute-done | bytes 262176 | tf_op jit(solution)/shard_map/ppermute | solution.py:24
  343.8 13.5 %attend_grad.1 = (bf16[256,512]{1,0:T(8,128)(2,1)}, bf16[1024,512]{1,0:T(8,128)(2,1)}) custom-call(s32[4]{0:T(128)} %pad_add_fusion.sc, bf16[128,1024]{1,0:T(8,128)(2,1)} %get-tuple-element.103.b0_ref.refs_0_, bf16[128,1024]{1,0:T(8,128)(2,1)} %copy-done.51, bf16[256,512]{1,0:T(8,128)(2,1)} %get-tuple-element.75.q_ref, bf16[1024,512]{1,0:T(8,128)(2,1)} %bitcast.47, ...), custom_call_target="tpu_custom_call" | custom-call | flops 1610612736 | bytes 5242880 | tf_op jit(solution)/shard_map/attend_grad/pallas_call | solution.py:585
  383.0 21.4 %collective-permute-done.57 = bf16[256,512]{1,0:T(8,128)(2,1)S(1)} collective-permute-done((bf16[256,512]{1,0:T(8,128)(2,1)S(1)}, bf16[256,512]{1,0:T(8,128)(2,1)S(1)}, u32[]{:S(2)}, u32[]{:S(2)}) %collective-permute-start.57) | collective-permute-done | bytes 262176 | tf_op jit(solution)/shard_map/ppermute | solution.py:24
  412.8 5.3 %back.1 = (f32[128,1024]{1,0:T(8,128)}, bf16[128,1024]{1,0:T(8,128)(2,1)}, f32[256,512]{1,0:T(8,128)}, bf16[256,512]{1,0:T(8,128)(2,1)}, f32[256,512]{1,0:T(8,128)}, /*index=5*/bf16[256,512]{1,0:T(8,128)(2,1)}) custom-call(s32[4]{0:T(128)} %pad_add_fusion.sc, bf16[256,512]{1,0:T(8,128)(2,1)} %get-tuple-element.105.dq_ref.refs_1_, ...), custom_call_target="tpu_custom_call" | custom-call | flops 805306368 | bytes 6291456 | tf_op jit(solution)/shard_map/back/pallas_call | solution.py:706
  430.8 6.0 %all-to-all-done.8 = bf16[4,64,640]{2,1,0:T(8,128)(2,1)S(1)} async-done(((bf16[4,64,640]{2,1,0:T(8,128)(2,1)}), bf16[4,64,640]{2,1,0:T(8,128)(2,1)S(1)}, u32[]{:S(2)}, u32[]{:S(2)}) %all-to-all-start.8) | async-done | bytes 327712 | tf_op jit(solution)/shard_map/all_to_all | solution.py:672
  (328 shorter events, 156.5 us)
Async XLA Ops:
  93.5 28.7 %all-to-all-start.3 = ((bf16[4,128,1024]{2,1,0:T(8,128)(2,1)}), bf16[4,128,1024]{2,1,0:T(8,128)(2,1)}, u32[]{:S(2)}, u32[]{:S(2)}) async-start(bf16[4,128,1024]{2,1,0:T(8,128)(2,1)} %broadcast_in_dim.29), calls=%async_computation.3 | async-start | bytes 2097152 | tf_op jit(solution)/shard_map/all_to_all | solution.py:30
  123.7 38.8 %collective-permute-start.15 = (bf16[4,3,256,256]{3,2,1,0:T(8,128)(2,1)}, bf16[4,3,256,256]{3,2,1,0:T(8,128)(2,1)}, u32[]{:S(2)}, u32[]{:S(2)}) collective-permute-start(bf16[4,3,256,256]{3,2,1,0:T(8,128)(2,1)} %get-tuple-element.85.refs_10_), channel_id=1, source_target_pairs={{0,16},{8,24},{16,0},{24,8},{1,17},{9,25},{17,1},{25,9},{2,18},{10... | collective-permute-start | bytes 4718600 | tf_op jit(solution)/shard_map/ppermute | solution.py:24
  125.3 67.6 %collective-permute-start.16 = (bf16[4,3,256,256]{3,2,1,0:T(8,128)(2,1)S(1)}, bf16[4,3,256,256]{3,2,1,0:T(8,128)(2,1)}, u32[]{:S(2)}, u32[]{:S(2)}) collective-permute-start(bf16[4,3,256,256]{3,2,1,0:T(8,128)(2,1)S(1)} %collective-permute-done.14.refs_11_), channel_id=1, source_target_pairs={{0,16},{8,24},{16,0},{24,8},{1,17},{9,25},{17,1},{25,9},{2,18},{10... | collective-permute-start | bytes 4718600 | tf_op jit(solution)/shard_map/ppermute | solution.py:24
  139.4 68.0 %collective-permute-start.11 = (bf16[4,128,1024]{2,1,0:T(8,128)(2,1)}, bf16[4,128,1024]{2,1,0:T(8,128)(2,1)S(1)}, u32[]{:S(2)}, u32[]{:S(2)}) collective-permute-start(bf16[4,128,1024]{2,1,0:T(8,128)(2,1)} %all-to-all-done.3.refs_4_), channel_id=1, source_target_pairs={{0,8},{8,0},{16,24},{24,16},{1,9},{9,1},{17,25},{25,17},{2,10},{10... | collective-permute-start | bytes 3145736 | tf_op jit(solution)/shard_map/ppermute | solution.py:24
  148.6 60.3 %collective-permute-start.12 = (bf16[4,128,1024]{2,1,0:T(8,128)(2,1)}, bf16[4,128,1024]{2,1,0:T(8,128)(2,1)S(1)}, u32[]{:S(2)}, u32[]{:S(2)}) collective-permute-start(bf16[4,128,1024]{2,1,0:T(8,128)(2,1)} %collective-permute-done.10.refs_5_), channel_id=1, source_target_pairs={{0,8},{8,0},{16,24},{24,16},{1,9},{9,1},{17,25},{25,17},{2,10},{10... | collective-permute-start | bytes 3145736 | tf_op jit(solution)/shard_map/ppermute | solution.py:24
  160.7 32.2 %collective-permute-start.33 = (bf16[128,1024]{1,0:T(8,128)(2,1)}, bf16[128,1024]{1,0:T(8,128)(2,1)S(1)}, u32[]{:S(2)}, u32[]{:S(2)}) collective-permute-start(bf16[128,1024]{1,0:T(8,128)(2,1)} %get-tuple-element.83.refs_0_), channel_id=1, source_target_pairs={{0,6},{2,4},{4,2},{6,0},{1,7},{3,5},{5,3},{7,1},{8,14},{10,12},{12... | collective-permute-start | bytes 786440 | tf_op jit(solution)/shard_map/ppermute | solution.py:24
  162.5 31.0 %collective-permute-start.26 = (bf16[128,1024]{1,0:T(8,128)(2,1)}, bf16[128,1024]{1,0:T(8,128)(2,1)S(1)}, u32[]{:S(2)}, u32[]{:S(2)}) collective-permute-start(bf16[128,1024]{1,0:T(8,128)(2,1)} %get-tuple-element.83.refs_0_), channel_id=1, source_target_pairs={{0,4},{2,6},{4,0},{6,2},{1,5},{3,7},{5,1},{7,3},{8,12},{10,14},{12... | collective-permute-start | bytes 786440 | tf_op jit(solution)/shard_map/ppermute | solution.py:24
  200.0 52.4 %collective-permute-start.8 = (bf16[128,1024]{1,0:T(8,128)(2,1)}, bf16[128,1024]{1,0:T(8,128)(2,1)S(1)}, u32[]{:S(2)}, u32[]{:S(2)}) collective-permute-start(bf16[128,1024]{1,0:T(8,128)(2,1)} %get-tuple-element.83.refs_0_), channel_id=1, source_target_pairs={{0,8},{8,0},{16,24},{24,16},{1,9},{9,1},{17,25},{25,17},{2,10},{10... | collective-permute-start | bytes 786440 | tf_op jit(solution)/shard_map/ppermute | solution.py:24
  223.5 29.2 %collective-permute-start.9 = (bf16[128,1024]{1,0:T(8,128)(2,1)S(1)}, bf16[128,1024]{1,0:T(8,128)(2,1)S(1)}, u32[]{:S(2)}, u32[]{:S(2)}) collective-permute-start(bf16[128,1024]{1,0:T(8,128)(2,1)S(1)} %collective-permute-done.7.refs_1_), channel_id=1, source_target_pairs={{0,8},{8,0},{16,24},{24,16},{1,9},{9,1},{17,25},{25,17},{2,10},{10... | collective-permute-start | bytes 786440 | tf_op jit(solution)/shard_map/ppermute | solution.py:24
  224.0 54.4 %collective-permute-start.37 = (bf16[256,1024]{1,0:T(8,128)(2,1)}, bf16[256,1024]{1,0:T(8,128)(2,1)S(1)}, u32[]{:S(2)}, u32[]{:S(2)}) collective-permute-start(bf16[256,1024]{1,0:T(8,128)(2,1)} %get-tuple-element.94), channel_id=1, source_target_pairs={{0,8},{8,0},{16,24},{24,16},{1,9},{9,1},{17,25},{25,17},{2,10},{10... | collective-permute-start | bytes 1572872 | tf_op jit(solution)/shard_map/ppermute | solution.py:24
  238.1 40.8 %collective-permute-start.49 = (bf16[256,1024]{1,0:T(8,128)(2,1)S(1)}, bf16[256,1024]{1,0:T(8,128)(2,1)S(1)}, u32[]{:S(2)}, u32[]{:S(2)}) collective-permute-start(bf16[256,1024]{1,0:T(8,128)(2,1)S(1)} %copy-done.41), channel_id=1, source_target_pairs={{0,8},{8,0},{16,24},{24,16},{1,9},{9,1},{17,25},{25,17},{2,10},{10... | collective-permute-start | bytes 1572872 | tf_op jit(solution)/shard_map/ppermute | solution.py:24
  238.5 40.7 %collective-permute-start.30 = (bf16[256,1024]{1,0:T(8,128)(2,1)}, bf16[256,1024]{1,0:T(8,128)(2,1)S(1)}, u32[]{:S(2)}, u32[]{:S(2)}) collective-permute-start(bf16[256,1024]{1,0:T(8,128)(2,1)} %get-tuple-element.92), channel_id=1, source_target_pairs={{0,8},{8,0},{16,24},{24,16},{1,9},{9,1},{17,25},{25,17},{2,10},{10... | collective-permute-start | bytes 1572872 | tf_op jit(solution)/shard_map/ppermute | solution.py:24
  252.5 28.1 %collective-permute-start.46 = (bf16[256,1024]{1,0:T(8,128)(2,1)S(1)}, bf16[256,1024]{1,0:T(8,128)(2,1)S(1)}, u32[]{:S(2)}, u32[]{:S(2)}) collective-permute-start(bf16[256,1024]{1,0:T(8,128)(2,1)S(1)} %copy-done.42), channel_id=1, source_target_pairs={{0,8},{8,0},{16,24},{24,16},{1,9},{9,1},{17,25},{25,17},{2,10},{10... | collective-permute-start | bytes 1572872 | tf_op jit(solution)/shard_map/ppermute | solution.py:24
  252.7 28.5 %collective-permute-start.23 = (bf16[256,1024]{1,0:T(8,128)(2,1)}, bf16[256,1024]{1,0:T(8,128)(2,1)S(1)}, u32[]{:S(2)}, u32[]{:S(2)}) collective-permute-start(bf16[256,1024]{1,0:T(8,128)(2,1)} %get-tuple-element.90), channel_id=1, source_target_pairs={{0,8},{8,0},{16,24},{24,16},{1,9},{9,1},{17,25},{25,17},{2,10},{10... | collective-permute-start | bytes 1572872 | tf_op jit(solution)/shard_map/ppermute | solution.py:24
  280.6 37.6 %collective-permute-start.38 = (bf16[128,1024]{1,0:T(8,128)(2,1)S(1)}, bf16[128,1024]{1,0:T(8,128)(2,1)S(1)}, u32[]{:S(2)}, u32[]{:S(2)}) collective-permute-start(bf16[128,1024]{1,0:T(8,128)(2,1)S(1)} %add_convert_fusion.16), channel_id=1, source_target_pairs={{0,1},{1,0},{2,3},{3,2},{4,5},{5,4},{6,7},{7,6},{8,9},{9,8},{10,11... | collective-permute-start | bytes 786440 | tf_op jit(solution)/shard_map/ppermute | solution.py:24
  283.5 51.8 %collective-permute-start.31 = (bf16[128,1024]{1,0:T(8,128)(2,1)}, bf16[128,1024]{1,0:T(8,128)(2,1)S(1)}, u32[]{:S(2)}, u32[]{:S(2)}) collective-permute-start(bf16[128,1024]{1,0:T(8,128)(2,1)} %add_convert_fusion.18), channel_id=1, source_target_pairs={{0,1},{1,0},{2,3},{3,2},{4,5},{5,4},{6,7},{7,6},{8,9},{9,8},{10,11... | collective-permute-start | bytes 786440 | tf_op jit(solution)/shard_map/ppermute | solution.py:24
  318.8 57.7 %collective-permute-start.67 = (bf16[4,3,256,256]{3,2,1,0:T(8,128)(2,1)}, bf16[4,3,256,256]{3,2,1,0:T(8,128)(2,1)S(1)}, u32[]{:S(2)}, u32[]{:S(2)}) collective-permute-start(bf16[4,3,256,256]{3,2,1,0:T(8,128)(2,1)} %get-tuple-element.140), channel_id=1, source_target_pairs={{0,16},{8,24},{16,0},{24,8},{1,17},{9,25},{17,1},{25,9},{2,18},{10... | collective-permute-start | bytes 4718600 | tf_op jit(solution)/shard_map/ppermute | solution.py:24
  330.9 30.3 %collective-permute-start.18 = (bf16[128,1024]{1,0:T(8,128)(2,1)}, bf16[128,1024]{1,0:T(8,128)(2,1)}, u32[]{:S(2)}, u32[]{:S(2)}) collective-permute-start(bf16[128,1024]{1,0:T(8,128)(2,1)} %add_convert_fusion.21), channel_id=1, source_target_pairs={{0,1},{1,0},{2,3},{3,2},{4,5},{5,4},{6,7},{7,6},{8,9},{9,8},{10,11... | collective-permute-start | bytes 786440 | tf_op jit(solution)/shard_map/ppermute | solution.py:24
  330.9 32.0 %collective-permute-start.39 = (bf16[128,1024]{1,0:T(8,128)(2,1)S(1)}, bf16[128,1024]{1,0:T(8,128)(2,1)}, u32[]{:S(2)}, u32[]{:S(2)}) collective-permute-start(bf16[128,1024]{1,0:T(8,128)(2,1)S(1)} %add_convert_fusion.15), channel_id=1, source_target_pairs={{0,6},{2,4},{4,2},{6,0},{1,7},{3,5},{5,3},{7,1},{8,14},{10,12},{12... | collective-permute-start | bytes 786440 | tf_op jit(solution)/shard_map/ppermute | solution.py:24
  357.3 48.0 %all-to-all-start.5 = ((bf16[4,256,512]{2,1,0:T(8,128)(2,1)}), bf16[4,256,512]{2,1,0:T(8,128)(2,1)S(1)}, u32[]{:S(2)}, u32[]{:S(2)}) async-start(bf16[4,256,512]{2,1,0:T(8,128)(2,1)} %bitcast.49), calls=%async_computation.5 | async-start | bytes 2097152 | tf_op jit(solution)/shard_map/all_to_all | solution.py:924
  361.3 48.8 %collective-permute-start.66 = (bf16[4,3,256,256]{3,2,1,0:T(8,128)(2,1)}, bf16[4,3,256,256]{3,2,1,0:T(8,128)(2,1)}, u32[]{:S(2)}, u32[]{:S(2)}) collective-permute-start(bf16[4,3,256,256]{3,2,1,0:T(8,128)(2,1)} %get-tuple-element.138), channel_id=1, source_target_pairs={{0,16},{8,24},{16,0},{24,8},{1,17},{9,25},{17,1},{25,9},{2,18},{10... | collective-permute-start | bytes 4718600 | tf_op jit(solution)/shard_map/ppermute | solution.py:24
  373.0 45.1 %collective-permute-start.62 = (bf16[256,640]{1,0:T(8,128)(2,1)}, bf16[256,640]{1,0:T(8,128)(2,1)}, u32[]{:S(2)}, u32[]{:S(2)}) collective-permute-start(bf16[256,640]{1,0:T(8,128)(2,1)} %get-tuple-element.122), channel_id=1, source_target_pairs={{0,8},{8,0},{16,24},{24,16},{1,9},{9,1},{17,25},{25,17},{2,10},{10... | collective-permute-start | bytes 983048 | tf_op jit(solution)/shard_map/ppermute | solution.py:24
  380.6 66.8 %collective-permute-start.68 = (bf16[4,3,256,256]{3,2,1,0:T(8,128)(2,1)}, bf16[4,3,256,256]{3,2,1,0:T(8,128)(2,1)}, u32[]{:S(2)}, u32[]{:S(2)}) collective-permute-start(bf16[4,3,256,256]{3,2,1,0:T(8,128)(2,1)} %add_convert_fusion), channel_id=1, source_target_pairs={{0,8},{8,0},{16,24},{24,16},{1,9},{9,1},{17,25},{25,17},{2,10},{10... | collective-permute-start | bytes 4718600 | tf_op jit(solution)/shard_map/ppermute | solution.py:24
  381.4 36.8 %collective-permute-start.64 = (bf16[256,640]{1,0:T(8,128)(2,1)}, bf16[256,640]{1,0:T(8,128)(2,1)}, u32[]{:S(2)}, u32[]{:S(2)}) collective-permute-start(bf16[256,640]{1,0:T(8,128)(2,1)} %add_convert_fusion.2), channel_id=1, source_target_pairs={{0,16},{8,24},{16,0},{24,8},{1,17},{9,25},{17,1},{25,9},{2,18},{10... | collective-permute-start | bytes 983048 | tf_op jit(solution)/shard_map/ppermute | solution.py:24
  (115 other events, 1308.6 us)

commit v2 on v1

v2 whole, which is shorter than its diff:
```python
import functools

import jax
import jax.numpy as jnp
from jax import lax
from jax.experimental import pallas as pl
from jax.experimental.pallas import tpu as pltpu
from jax.sharding import PartitionSpec as P

HEAD_DIM = 64
EXPERTS = 32
TOPK = 8
PIECE = 256
CAP = 96
EPS = 1e-06
MASKED = -1e30
LANES = 128
F32 = jnp.float32
BF16 = jnp.bfloat16


def swap(value, axis, distance):
    size = lax.axis_size(axis)
    return lax.ppermute(value, axis, [(i, i ^ distance) for i in range(size)])


def spread(value, axis):
    size = lax.axis_size(axis)
    copies = jnp.broadcast_to(value[None], (size,) + value.shape)
    return lax.all_to_all(copies, axis, 0, 0, tiled=True)


def after(value, *others):
    return lax.optimization_barrier((value,) + others)[0]


def fence(*values):
    return lax.optimization_barrier(values)


def dot_nn(a, b):
    return lax.dot_general(a, b, (((1,), (0,)), ((), ())), preferred_element_type=F32)


def dot_nt(a, b):
    return lax.dot_general(a, b, (((1,), (1,)), ((), ())), preferred_element_type=F32)


def dot_tn(a, b):
    return lax.dot_general(a, b, (((0,), (0,)), ((), ())), preferred_element_type=F32)


def cost(flops, moved, special=0):
    return pl.CostEstimate(flops=int(flops), bytes_accessed=int(moved), transcendentals=int(special))


def params(megabytes, length=0):
    megabytes = 58 if length > 1024 else megabytes
    return pltpu.CompilerParams(vmem_limit_bytes=megabytes * 1024 * 1024)


def sds(shape, dtype):
    return jax.ShapeDtypeStruct(shape, dtype)


def whole(shape):
    return pl.BlockSpec(shape, lambda *_: (0,) * len(shape))


def turn(value, cosine, sine):
    lane = lax.broadcasted_iota(jnp.int32, (value.shape[0], LANES), 1) % HEAD_DIM
    first = lane < HEAD_DIM // 2
    parts = []
    for j in range(value.shape[1] // LANES):
        chunk = value[:, j * LANES : (j + 1) * LANES]
        partner = jnp.where(
            first,
            pltpu.roll(chunk, LANES - HEAD_DIM // 2, 1),
            pltpu.roll(chunk, HEAD_DIM // 2, 1),
        )
        parts.append(chunk * cosine + partner * sine)
    return parts[0] if len(parts) == 1 else jnp.concatenate(parts, axis=1)


def rows_at(index, size):
    return pl.ds(pl.multiple_of(index * size, size), size)


def columns(scalars, p, width):
    return pl.ds(pl.multiple_of((scalars[0] ^ p) * width, width), width)


def front(scalars, layer_input, others, pieces, cos_table, sin_table, widths):
    tokens, model = layer_input.shape
    quarter = pieces[0].shape[0]
    q_width, kv_width = widths
    heads = q_width + 2 * kv_width
    gain_column = pieces[0].shape[1] - LANES
    half = tokens // 2
    count = len(pieces)
    groups = 1 + len(others) // 2
    length = groups * tokens

    def body(sc, x_ref, *rest):
        other_refs, rest = rest[: len(others)], rest[len(others) :]
        piece_refs = rest[:count]
        cos_ref, sin_ref, xn_ref, q_ref, kv_ref, gain_ref = rest[count:]
        rows = lax.broadcasted_iota(jnp.int32, (quarter, quarter), 0)
        diagonal = rows == lax.broadcasted_iota(jnp.int32, (quarter, quarter), 1)
        for p in range(count):
            gains = piece_refs[p][:, gain_column : gain_column + LANES].astype(F32)
            for k in range(2):
                row = jnp.sum(jnp.where(diagonal, gains[:, k : k + 1], 0.0), axis=0, keepdims=True)
                gain_ref[k : k + 1, columns(sc, p, quarter)] = row
        gain = gain_ref[0:1, :]
        for b in range(groups):
            for h in range(2):
                if b == 0:
                    values = x_ref[rows_at(sc[2] ^ h, half)].astype(F32)
                else:
                    values = other_refs[2 * (b - 1) + h][...].astype(F32)
                inverse = lax.rsqrt(jnp.mean(values * values, axis=-1, keepdims=True) + EPS)
                xn_ref[rows_at(2 * (sc[1] ^ b) + h, half)] = (values * inverse * gain).astype(BF16)

        own = rows_at(sc[1], tokens)
        total = None
        for p in range(count):
            part = dot_nn(xn_ref[own, columns(sc, p, quarter)], piece_refs[p][:, :q_width])
            total = part if total is None else total + part
        total = turn(total, cos_ref[own], sin_ref[own]).astype(BF16)
        q_ref[...] = (total * HEAD_DIM**-0.5).astype(BF16)

        @pl.loop(0, groups)
        def _(g):
            here = rows_at(g, tokens)
            total = None
            for p in range(count):
                part = dot_nn(xn_ref[here, columns(sc, p, quarter)], piece_refs[p][:, q_width:heads])
                total = part if total is None else total + part
            kv_ref[here, :kv_width] = turn(total[:, :kv_width], cos_ref[here], sin_ref[here]).astype(
                BF16
            )
            kv_ref[here, kv_width:] = total[:, kv_width:].astype(BF16)

    outs = [
        ((length, model), BF16),
        ((tokens, q_width), BF16),
        ((length, 2 * kv_width), BF16),
        ((8, model), F32),
    ]
    arrays = (layer_input, *others, *pieces, cos_table, sin_table)
    return pl.pallas_call(
        body,
        out_shape=[sds(*o) for o in outs],
        grid_spec=pltpu.PrefetchScalarGridSpec(
            num_scalar_prefetch=1,
            grid=(1,),
            in_specs=[whole(a.shape) for a in arrays],
            out_specs=[whole(o[0]) for o in outs],
        ),
        compiler_params=params(58),
        cost_estimate=cost(
            2 * model * (tokens * q_width + length * 2 * kv_width),
            2 * model * (2 * length + heads) + 2 * length * (kv_width + 2 * LANES),
        ),
        name="front",
    )(scalars, *arrays)


def inside_piece(position, start):
    return (position >= start) & (position < start + PIECE)


def seen_bias(sc, query_pos, key_pos, piece_count):
    seen = key_pos <= query_pos
    for k in range(piece_count):
        start = sc[3 + k]
        seen = seen | (inside_piece(query_pos, start) & inside_piece(key_pos, start))
    return jnp.where(seen, 0.0, MASKED)


def token_position(sc, index, group, tokens):
    return group * tokens + (index ^ (sc[2] * (tokens // 2)))


def attend(scalars, queries, kv_all, out_pieces, piece_count):
    tokens, q_width = queries.shape
    length, kv2 = kv_all.shape
    kv_width = kv2 // 2
    kv_heads = kv_width // HEAD_DIM
    heads = q_width + kv2
    pair_blocks = kv_width // LANES
    count = len(out_pieces)
    quarter = out_pieces[0].shape[0]
    model = quarter * count
    half = tokens // 2

    def body(sc, q_ref, k_ref, v_ref, *rest):
        out_refs = rest[:count]
        mixed_ref, lse_ref, own_ref, send_ref, bias_ref = rest[count:]
        c = pl.program_id(0)

        @pl.when(c == 0)
        def _():
            rows = lax.broadcasted_iota(jnp.int32, (tokens, length), 0)
            cols = lax.broadcasted_iota(jnp.int32, (tokens, length), 1)
            query_pos = token_position(sc, rows, sc[1], tokens)
            key_pos = token_position(sc, cols % tokens, cols // tokens, tokens)
            bias_ref[...] = seen_bias(sc, query_pos, key_pos, piece_count)

        low = lax.broadcasted_iota(jnp.int32, (1, LANES), 1) < HEAD_DIM
        mine = low == (c % 2 == 0)
        keys = k_ref[...].astype(F32)
        keys = jnp.where(mine, keys, pltpu.roll(keys, HEAD_DIM, 1)).astype(BF16)
        vals = v_ref[...].astype(F32)
        vals = jnp.where(mine, vals, pltpu.roll(vals, HEAD_DIM, 1)).astype(BF16)
        query = q_ref[...]
        zero = jnp.zeros_like(query)
        outs, lses = [], []
        for part in (jnp.where(low, query, zero), jnp.where(low, zero, query)):
            scores = dot_nt(part, keys) + bias_ref[...]
            top = jnp.max(scores, axis=-1, keepdims=True)
            expo = jnp.exp(scores - top)
            total = jnp.sum(expo, axis=-1, keepdims=True)
            probs = expo * (1.0 / total)
            outs.append(dot_nn(probs.astype(BF16), vals))
            lses.append(top + jnp.log(total))
        mixed_ref[:, pl.ds(pl.multiple_of(c * LANES, LANES), LANES)] = jnp.where(
            low, outs[0], outs[1]
        ).astype(BF16)
        lse_ref[...] = jnp.where(low, lses[0], lses[1])

        @pl.when(c == kv_heads - 1)
        def _():
            mixed = mixed_ref[...]
            for p in range(count):
                part = dot_nt(mixed, out_refs[p][...])
                own_ref[:, columns(sc, p, quarter)] = part[:half]
                send_ref[:, columns(sc, p, quarter)] = part[half:].astype(BF16)

    return pl.pallas_call(
        body,
        out_shape=[
            sds((tokens, q_width), BF16),
            sds((tokens, kv_heads * LANES), F32),
            sds((half, model), F32),
            sds((half, model), BF16),
        ],
        grid_spec=pltpu.PrefetchScalarGridSpec(
            num_scalar_prefetch=1,
            grid=(kv_heads,),
            in_specs=[
                pl.BlockSpec((tokens, LANES), lambda c, sc: (0, c)),
                pl.BlockSpec((length, LANES), lambda c, sc: (0, c // 2)),
                pl.BlockSpec((length, LANES), lambda c, sc: (0, pair_blocks + c // 2)),
            ]
            + [pl.BlockSpec((quarter, q_width), lambda c, sc: (0, heads // q_width))] * count,
            out_specs=[
                whole((tokens, q_width)),
                pl.BlockSpec((tokens, LANES), lambda c, sc: (0, c)),
                whole((half, model)),
                whole((half, model)),
            ],
            scratch_shapes=[pltpu.VMEM((tokens, length), F32)],
        ),
        compiler_params=params(58),
        cost_estimate=cost(
            16 * tokens * length * LANES + 2 * tokens * q_width * model,
            4 * length * kv2 + 8 * tokens * model,
            2 * kv_heads * tokens * length,
        ),
        name="attend",
    )(scalars, queries, kv_all, kv_all, *out_pieces)


def second_norm(scalars, layer_input, own, received, gains):
    tokens, model = layer_input.shape
    half = tokens // 2

    def body(sc, x_ref, own_ref, rec_ref, gain_ref, res_ref, norm_ref):
        start = pl.multiple_of(sc[2] * half, half)
        residual = (
            x_ref[pl.ds(start, half)].astype(F32) + own_ref[...] + rec_ref[...].astype(F32)
        )
        inverse = lax.rsqrt(jnp.mean(residual * residual, axis=-1, keepdims=True) + EPS)
        res_ref[...] = residual
        norm_ref[...] = (residual * inverse * gain_ref[1:2, :]).astype(BF16)

    return pl.pallas_call(
        body,
        out_shape=[sds((half, model), F32), sds((half, model), BF16)],
        grid_spec=pltpu.PrefetchScalarGridSpec(
            num_scalar_prefetch=1,
            grid=(1,),
            in_specs=[
                whole((tokens, model)),
                whole((half, model)),
                whole((half, model)),
                whole((8, model)),
            ],
            out_specs=[whole((half, model)), whole((half, model))],
        ),
        compiler_params=params(8),
        cost_estimate=cost(10 * half * model, 16 * half * model),
        name="second_norm",
    )(scalars, layer_input, own, received, gains)


def experts(scalars, fars, rows_in, grads_in, weights):
    k, _, half, model = rows_in[0].shape
    tokens = 2 * half
    local, quarter, hidden = weights[0].shape
    count = model // quarter
    per_group = 2 * local
    blocks = [(side, g) for side in range(2) for g in range(k)]
    rows_each = len(blocks) * CAP

    def body(sc, *refs):
        x_refs, refs = refs[:2], refs[2:]
        g_refs, refs = refs[:2], refs[2:]
        w_refs, refs = refs[: len(weights)], refs[len(weights) :]
        na_ref, nb_ref, ya_ref, yb_ref, h_ref, d_out, go_out = refs[:7]
        st_ref, gate_ref, ns_ref, ys_ref, d_ref, go_ref, sems = refs[7:]

        def weight(p, e, m):
            return w_refs[3 * p + m][e]

        copies = (
            pltpu.make_async_copy(d_ref, d_out, sems.at[0]),
            pltpu.make_async_copy(go_ref, go_out, sems.at[1]),
        )
        base = sc[1] * per_group + (sc[0] % 2) * local
        slot_row = lax.broadcasted_iota(jnp.int32, (CAP, tokens), 0).astype(F32)
        for n, (side, g) in enumerate(blocks):
            place = sc[1] ^ fars[g]
            rows = slice(n * CAP, (n + 1) * CAP)
            table = g_refs[side][place, :, model : model + LANES].astype(F32).T
            ids, slots = table[:TOPK], table[TOPK : 2 * TOPK] - CAP
            gates = table[2 * TOPK : 3 * TOPK] + table[3 * TOPK : 4 * TOPK]
            picks = []
            for e in range(local):
                hit = ids == (base + e).astype(F32)
                slot = jnp.sum(jnp.where(hit, slots, 0.0), axis=0, keepdims=True) + CAP
                gate = jnp.sum(jnp.where(hit, gates, 0.0), axis=0, keepdims=True)
                pick = slot_row == slot
                value = jnp.sum(jnp.where(pick, gate, 0.0), axis=1, keepdims=True)
                gate_ref[e, rows, :] = jnp.broadcast_to(value, (CAP, LANES))
                picks.append(jnp.where(pick, 1.0, 0.0))
            pick = jnp.concatenate(picks, axis=0)
            st_ref[n] = pick.T.astype(BF16)
            pick = pick.astype(BF16)
            for p in range(count):
                cols = columns(sc, p, quarter)
                values = jnp.concatenate(
                    [x_refs[side][g, 0, :, cols], x_refs[side][g, 1, :, cols]], axis=0
                )
                got = dot_nn(pick, values).astype(BF16)
                grad = dot_nn(pick, g_refs[side][place, :, cols])
                for e in range(local):
                    here = slice(e * CAP, (e + 1) * CAP)
                    d_ref[e, rows, p * quarter : (p + 1) * quarter] = got[here]
                    go_ref[e, rows, p * quarter : (p + 1) * quarter] = (
                        grad[here] * gate_ref[e, rows, 0:1]
                    ).astype(BF16)
        for copy in copies:
            copy.start()

        @pl.loop(0, local)
        def _(e):
            gate = up = act_grad = None
            for p in range(count):
                cols = slice(p * quarter, (p + 1) * quarter)
                rows = d_ref[e, :, cols]
                a = dot_nn(rows, weight(p, e, 0))
                b = dot_nn(rows, weight(p, e, 1))
                c = dot_nn(go_ref[e, :, cols], weight(p, e, 2))
                gate = a if gate is None else gate + a
                up = b if up is None else up + b
                act_grad = c if act_grad is None else act_grad + c
            sig = jax.nn.sigmoid(gate)
            silu = gate * sig
            act = (silu * up).astype(BF16)
            up_grad = (act_grad * silu).astype(BF16)
            gate_grad = (act_grad * up * sig * (1.0 + gate * (1.0 - sig))).astype(BF16)
            h_ref[e, :, :hidden] = act
            h_ref[e, :, hidden : 2 * hidden] = gate_grad
            h_ref[e, :, 2 * hidden :] = up_grad
            scale = gate_ref[e, :, 0:1]
            for p in range(count):
                cols = slice(p * quarter, (p + 1) * quarter)
                ns_ref[e, :, cols] = (
                    dot_nt(gate_grad, weight(p, e, 0)) + dot_nt(up_grad, weight(p, e, 1))
                ).astype(BF16)
                ys_ref[e, :, cols] = (dot_nt(act, weight(p, e, 2)) * scale).astype(BF16)

        for n, (side, g) in enumerate(blocks):
            place = st_ref[n]
            rows = slice(n * CAP, (n + 1) * CAP)
            for p in range(count):
                cols = slice(p * quarter, (p + 1) * quarter)
                target = columns(sc, p, quarter)
                for source, out in ((ns_ref, (na_ref, nb_ref)), (ys_ref, (ya_ref, yb_ref))):
                    stacked = jnp.concatenate([source[e, rows, cols] for e in range(local)], axis=0)
                    out[side][g, :, target] = dot_nn(place, stacked).astype(BF16)
        for copy in copies:
            copy.wait()

    anywhere = pl.BlockSpec(memory_space=pl.ANY)
    resident = pl.BlockSpec(memory_space=pltpu.VMEM)
    sums = sds((k, tokens, model), BF16)
    rows = sds((local, rows_each, model), BF16)
    return pl.pallas_call(
        body,
        out_shape=[sums] * 4 + [sds((local, rows_each, 3 * hidden), BF16), rows, rows],
        grid_spec=pltpu.PrefetchScalarGridSpec(
            num_scalar_prefetch=1,
            grid=(1,),
            in_specs=[resident] * (4 + len(weights)),
            out_specs=[resident] * 5 + [anywhere] * 2,
            scratch_shapes=[
                pltpu.VMEM((len(blocks), tokens, local * CAP), BF16),
                pltpu.VMEM((local, rows_each, LANES), F32),
                pltpu.VMEM((local, rows_each, model), BF16),
                pltpu.VMEM((local, rows_each, model), BF16),
                pltpu.VMEM((local, rows_each, model), BF16),
                pltpu.VMEM((local, rows_each, model), BF16),
                pltpu.SemaphoreType.DMA((2,)),
            ],
        ),
        compiler_params=params(30, 0),
        cost_estimate=cost(
            2 * local * rows_each * model * (6 * hidden + 4 * tokens),
            2 * 3 * count * local * quarter * hidden + 24 * k * tokens * model,
            local * rows_each * hidden,
        ),
        name="experts",
    )(scalars, *rows_in, *grads_in, *weights)


def expert_weight_grads(row_sets, grad_sets, hidden_sets, quarter):
    groups = len(row_sets)
    local, rows, model = row_sets[0].shape
    hidden = hidden_sets[0].shape[2] // 3
    count = model // quarter
    step = min(groups, 2)
    far_sizes = [(e, [2, 4] if e == 1 else [6]) for e in range(local)]

    def body(*refs):
        d_refs, go_refs, h_refs = refs[:groups], refs[groups : 2 * groups], refs[2 * groups : 3 * groups]
        keep_refs, far_refs = refs[3 * groups : 3 * groups + 2], refs[3 * groups + 2 :]
        expert = pl.program_id(0)
        far = []
        for p in range(count):
            cols = slice(p * quarter, (p + 1) * quarter)
            sums = [None, None, None]
            for start in range(0, groups, step):
                chosen = range(start, start + step)
                left = jnp.concatenate([d_refs[g][0, :, cols] for g in chosen], axis=0)
                left_out = jnp.concatenate([go_refs[g][0, :, cols] for g in chosen], axis=0)
                right = jnp.concatenate([h_refs[g][0] for g in chosen], axis=0)
                parts = (
                    dot_tn(left, right[:, hidden : 2 * hidden]),
                    dot_tn(left, right[:, 2 * hidden :]),
                    dot_tn(left_out, right[:, :hidden]),
                )
                sums = [a if b is None else a + b for a, b in zip(parts, sums)]
            for k in range(3):
                if p < 2:
                    keep_refs[p][0, k] = sums[k]
                else:
                    far.append(sums[k].astype(BF16))
        n = 0
        for e, sizes in far_sizes:
            mine = far_refs[n : n + len(sizes)]
            n += len(sizes)

            @pl.when(expert == e)
            def _():
                at = 0
                for ref, size in zip(mine, sizes):
                    for k in range(size):
                        ref[k] = far[at + k]
                    at += size

    by_expert = lambda shape: pl.BlockSpec((1,) + shape, lambda e: (e,) + (0,) * len(shape))
    fars = [(size, quarter, hidden) for _, sizes in far_sizes for size in sizes]
    return pl.pallas_call(
        body,
        out_shape=[sds((local, 3, quarter, hidden), F32)] * 2 + [sds(f, BF16) for f in fars],
        grid=(local,),
        in_specs=[by_expert((rows, model))] * (2 * groups)
        + [by_expert((rows, 3 * hidden))] * groups,
        out_specs=[by_expert((3, quarter, hidden))] * 2 + [whole(f) for f in fars],
        compiler_params=params(56),
        cost_estimate=cost(
            6 * local * rows * groups * model * hidden,
            2 * groups * local * rows * (2 * model + 3 * hidden) + 3 * local * 3 * model * hidden,
        ),
        name="expert_weight_grads",
    )(*row_sets, *grad_sets, *hidden_sets)


def middle_grad(scalars, parts, residual, grad_out, gains):
    tokens, model = grad_out.shape
    half = tokens // 2
    count = len(parts)

    def body(sc, *refs):
        part_refs = refs[:count]
        res_ref, go_ref, gain_ref, rg_ref, branch_ref, sum_ref = refs[count:]
        total = part_refs[0][...].astype(F32)
        for k in range(1, count):
            total = total + part_refs[k][...].astype(F32)
        residual = res_ref[...]
        start = pl.multiple_of(sc[2] * half, half)
        inverse = lax.rsqrt(jnp.mean(residual * residual, axis=-1, keepdims=True) + EPS)
        scaled = gain_ref[1:2, :] * total
        shift = jnp.mean(scaled * residual, axis=-1, keepdims=True)
        grad = (
            go_ref[pl.ds(start, half)].astype(F32)
            + inverse * scaled
            - residual * (inverse * inverse * inverse * shift)
        )
        rg_ref[...] = grad
        branch_ref[...] = grad.astype(BF16)
        sum_ref[...] = jnp.broadcast_to(
            jnp.sum(total * residual * inverse, axis=0, keepdims=True), (8, model)
        )

    return pl.pallas_call(
        body,
        out_shape=[sds((half, model), F32), sds((half, model), BF16), sds((8, model), F32)],
        grid_spec=pltpu.PrefetchScalarGridSpec(
            num_scalar_prefetch=1,
            grid=(1,),
            in_specs=[whole((half, model))] * (count + 1)
            + [whole((tokens, model)), whole((8, model))],
            out_specs=[whole((half, model)), whole((half, model)), whole((8, model))],
        ),
        compiler_params=params(12),
        cost_estimate=cost(20 * half * model, 24 * half * model),
        name="middle_grad",
    )(scalars, *parts, residual, grad_out, gains)


def attend_grad(scalars, branch, queries, kv_all, lse, out_pieces, cos_table, sin_table, piece_count):
    tokens, q_width = queries.shape
    length, kv2 = kv_all.shape
    kv_width = kv2 // 2
    kv_heads = kv_width // HEAD_DIM
    heads = q_width + kv2
    pair_blocks = kv_width // LANES
    count = len(out_pieces)
    quarter = out_pieces[0].shape[0]
    model = quarter * count
    half = tokens // 2

    def body(sc, b0_ref, b1_ref, q_ref, k_ref, v_ref, lse_ref, cos_ref, sin_ref, *rest):
        own = rows_at(sc[1], tokens)
        out_refs = rest[:count]
        dq_ref, dkv_ref, mg_ref, bias_ref = rest[count:]
        c = pl.program_id(0)

        @pl.when(c == 0)
        def _():
            cols = lax.broadcasted_iota(jnp.int32, (length, tokens), 0)
            rows = lax.broadcasted_iota(jnp.int32, (length, tokens), 1)
            query_pos = token_position(sc, rows, sc[1], tokens)
            key_pos = token_position(sc, cols % tokens, cols // tokens, tokens)
            bias_ref[...] = seen_bias(sc, query_pos, key_pos, piece_count)
            total = None
            for p in range(count):
                col = columns(sc, p, quarter)
                block = jnp.concatenate([b0_ref[:, col], b1_ref[:, col]], axis=0)
                part = dot_nn(block, out_refs[p][...])
                total = part if total is None else total + part
            mg_ref[...] = total.astype(BF16)

        low = lax.broadcasted_iota(jnp.int32, (1, LANES), 1) < HEAD_DIM
        mine = low == (c % 2 == 0)
        keys = k_ref[...].astype(F32)
        keys = jnp.where(mine, keys, pltpu.roll(keys, HEAD_DIM, 1)).astype(BF16)
        vals = v_ref[...].astype(F32)
        vals = jnp.where(mine, vals, pltpu.roll(vals, HEAD_DIM, 1)).astype(BF16)
        query = q_ref[...]
        grad = mg_ref[:, pl.ds(pl.multiple_of(c * LANES, LANES), LANES)]
        zero = jnp.zeros_like(query)
        lse_t = lse_ref[...].T
        dqs = []
        dk = dv = None
        for g in range(2):
            query_g = jnp.where(low, query, zero) if g == 0 else jnp.where(low, zero, query)
            grad_g = jnp.where(low, grad, zero) if g == 0 else jnp.where(low, zero, grad)
            scores = dot_nt(keys, query_g) + bias_ref[...]
            probs = jnp.exp(scores - lse_t[g * HEAD_DIM : g * HEAD_DIM + 1])
            prob_grad = dot_nt(vals, grad_g)
            delta = jnp.sum(probs * prob_grad, axis=0, keepdims=True)
            score_grad = (probs * (prob_grad - delta)).astype(BF16)
            dqs.append(dot_tn(score_grad, keys))
            dk_g = dot_nn(score_grad, query_g)
            dv_g = dot_nn(probs.astype(BF16), grad_g)
            dk = dk_g if dk is None else dk + dk_g
            dv = dv_g if dv is None else dv + dv_g
        dq = jnp.where(low, dqs[0], dqs[1]) * HEAD_DIM**-0.5
        dq_ref[...] = turn(dq, cos_ref[own], -sin_ref[own]).astype(BF16)
        dk = turn(dk, cos_ref[...], -sin_ref[...])
        for k, value in ((0, dk), (pair_blocks, dv)):
            value = (value + pltpu.roll(value, HEAD_DIM, 1)).astype(BF16)
            where = pl.ds(pl.multiple_of((k + c // 2) * LANES, LANES), LANES)
            dkv_ref[:, where] = jnp.where(mine, value, dkv_ref[:, where])

    return pl.pallas_call(
        body,
        out_shape=[sds((tokens, q_width), BF16), sds((length, kv2), BF16)],
        grid_spec=pltpu.PrefetchScalarGridSpec(
            num_scalar_prefetch=1,
            grid=(kv_heads,),
            in_specs=[
                whole((half, model)),
                whole((half, model)),
                pl.BlockSpec((tokens, LANES), lambda c, sc: (0, c)),
                pl.BlockSpec((length, LANES), lambda c, sc: (0, c // 2)),
                pl.BlockSpec((length, LANES), lambda c, sc: (0, pair_blocks + c // 2)),
                pl.BlockSpec((tokens, LANES), lambda c, sc: (0, c)),
                whole((length, LANES)),
                whole((length, LANES)),
            ]
            + [pl.BlockSpec((quarter, q_width), lambda c, sc: (0, heads // q_width))] * count,
            out_specs=[
                pl.BlockSpec((tokens, LANES), lambda c, sc: (0, c)),
                whole((length, kv2)),
            ],
            scratch_shapes=[
                pltpu.VMEM((tokens, q_width), BF16),
                pltpu.VMEM((length, tokens), F32),
            ],
        ),
        compiler_params=params(24, length),
        cost_estimate=cost(
            40 * tokens * length * LANES + 2 * tokens * q_width * model,
            6 * length * kv2 + 8 * tokens * model,
            2 * kv_heads * tokens * length,
        ),
        name="attend_grad",
    )(scalars, *branch, queries, kv_all, kv_all, lse, cos_table, sin_table, *out_pieces)


def store_pieces(p, value, kept_refs, send_ref):
    if p % 2 == 0:
        kept_refs[p // 2][...] = value
    else:
        send_ref[p // 2] = value.astype(BF16)


def piece_shapes(quarter, width):
    return [((quarter, width), F32), ((quarter, width), F32), ((2, quarter, width), BF16)]


def out_grads(scalars, branch, mixed, extra, quarter):
    tokens, width = mixed.shape
    model = branch[0].shape[1]
    count = model // quarter
    outs = piece_shapes(quarter, width + LANES)

    def body(sc, b0_ref, b1_ref, mixed_ref, extra_ref, own_ref, far_ref, send_ref):
        values = mixed_ref[...]
        rows = lax.broadcasted_iota(jnp.int32, (quarter, quarter), 0)
        diagonal = rows == lax.broadcasted_iota(jnp.int32, (quarter, quarter), 1)
        for p in range(count):
            cols = columns(sc, p, quarter)
            block = jnp.concatenate([b0_ref[:, cols], b1_ref[:, cols]], axis=0)
            column = jnp.sum(jnp.where(diagonal, extra_ref[0:1, cols], 0.0), axis=1, keepdims=True)
            value = jnp.concatenate(
                [dot_tn(block, values), jnp.broadcast_to(column, (quarter, LANES))], axis=1
            )
            store_pieces(p, value, (own_ref, far_ref), send_ref)

    arrays = (*branch, mixed, extra)
    return pl.pallas_call(
        body,
        out_shape=[sds(*o) for o in outs],
        grid_spec=pltpu.PrefetchScalarGridSpec(
            num_scalar_prefetch=1,
            grid=(1,),
            in_specs=[whole(a.shape) for a in arrays],
            out_specs=[whole(o[0]) for o in outs],
        ),
        compiler_params=params(16),
        cost_estimate=cost(
            2 * tokens * model * width, 2 * tokens * (model + width) + 3 * model * width
        ),
        name="out_grads",
    )(scalars, *arrays)


def qkv_grads(scalars, normed, dq, dkv, quarter):
    length, model = normed.shape
    tokens, q_width = dq.shape
    width = q_width + dkv.shape[1]
    count = model // quarter
    outs = piece_shapes(quarter, width)

    def body(sc, xn_ref, dq_ref, dkv_ref, own_ref, far_ref, send_ref):
        own = rows_at(sc[1], tokens)
        for p in range(count):
            cols = columns(sc, p, quarter)
            value = jnp.concatenate(
                [dot_tn(xn_ref[own, cols], dq_ref[...]), dot_tn(xn_ref[:, cols], dkv_ref[...])],
                axis=1,
            )
            store_pieces(p, value, (own_ref, far_ref), send_ref)

    arrays = (normed, dq, dkv)
    return pl.pallas_call(
        body,
        out_shape=[sds(*o) for o in outs],
        grid_spec=pltpu.PrefetchScalarGridSpec(
            num_scalar_prefetch=1,
            grid=(1,),
            in_specs=[whole(a.shape) for a in arrays],
            out_specs=[whole(o[0]) for o in outs],
        ),
        compiler_params=params(20, length),
        cost_estimate=cost(
            2 * model * (tokens * q_width + length * dkv.shape[1]),
            2 * length * (model + width) + 3 * model * width,
        ),
        name="qkv_grads",
    )(scalars, *arrays)


def over_mate(parts):
    own, far, sent = parts
    got = fence(swap(sent, "shard", 1))[0]
    return own + got[0].astype(F32), (far + got[1].astype(F32)).astype(BF16)


def over_ctx(kept, got):
    total = fence((kept + got.astype(F32)).astype(BF16))[0]
    groups = lax.axis_size("ctx")
    rows = total.shape[0] // groups
    return lax.all_to_all(total.reshape(groups, rows, total.shape[1]), "ctx", 0, 0, tiled=True)


def back(scalars, dq, dkv, pieces):
    tokens, q_width = dq.shape
    groups, _, kv2 = dkv.shape
    heads = q_width + kv2
    count = len(pieces)
    quarter = pieces[0].shape[0]
    model = count * quarter
    half = tokens // 2

    def body(sc, dq_ref, dkv_ref, *rest):
        piece_refs = rest[:count]
        own_ref, send_ref = rest[count:]
        total = dkv_ref[0].astype(F32)
        for g in range(1, groups):
            total = total + dkv_ref[g].astype(F32)
        dl_kv = total.astype(BF16)
        dl_q = dq_ref[...]
        for p in range(count):
            cols = columns(sc, p, quarter)
            part = dot_nt(dl_q, piece_refs[p][:, :q_width]) + dot_nt(
                dl_kv, piece_refs[p][:, q_width:heads]
            )
            own_ref[:, cols] = part[:half]
            send_ref[:, cols] = part[half:].astype(BF16)

    arrays = (dq, dkv, *pieces)
    return pl.pallas_call(
        body,
        out_shape=[sds((half, model), F32), sds((half, model), BF16)],
        grid_spec=pltpu.PrefetchScalarGridSpec(
            num_scalar_prefetch=1,
            grid=(1,),
            in_specs=[whole(dq.shape), whole(dkv.shape)] + [whole((quarter, heads))] * count,
            out_specs=[whole((half, model))] * 2,
        ),
        compiler_params=params(16, groups * tokens),
        cost_estimate=cost(2 * tokens * model * heads, 2 * model * (heads + 2 * tokens)),
        name="back",
    )(scalars, *arrays)


def last_grad(scalars, layer_input, own, received, residual_grad, gains):
    tokens, model = layer_input.shape
    half = tokens // 2

    def body(sc, x_ref, own_ref, rec_ref, rg_ref, gain_ref, out_ref):
        start = pl.multiple_of(sc[2] * half, half)
        values = x_ref[pl.ds(start, half)].astype(F32)
        inverse = lax.rsqrt(jnp.mean(values * values, axis=-1, keepdims=True) + EPS)
        scaled = gain_ref[0:1, :] * (own_ref[...] + rec_ref[...].astype(F32))
        shift = jnp.mean(scaled * values, axis=-1, keepdims=True)
        out_ref[...] = (
            rg_ref[...] + inverse * scaled - values * (inverse * inverse * inverse * shift)
        ).astype(BF16)

    return pl.pallas_call(
        body,
        out_shape=sds((half, model), BF16),
        grid_spec=pltpu.PrefetchScalarGridSpec(
            num_scalar_prefetch=1,
            grid=(1,),
            in_specs=[
                whole((tokens, model)),
                whole((half, model)),
                whole((half, model)),
                whole((half, model)),
                whole((8, model)),
            ],
            out_specs=whole((half, model)),
        ),
        compiler_params=params(8),
        cost_estimate=cost(12 * half * model, 14 * half * model),
        name="last_grad",
    )(scalars, layer_input, own, received, residual_grad, gains)


def local(
    layer_input,
    attn_norm,
    w_query,
    w_key,
    w_value,
    w_out,
    moe_norm,
    expert_weights,
    expert_ids,
    slot_ids,
    gate_values,
    piece_starts,
    grad_out,
):
    _, tokens, model = layer_input.shape
    half = tokens // 2
    groups = lax.axis_size("ctx")
    shard = lax.axis_index("shard")
    group = lax.axis_index("ctx")
    side = lax.axis_index("tp")
    piece_count = piece_starts.shape[1]
    scalars = jnp.concatenate(
        [jnp.stack([shard, group, side]).astype(jnp.int32), piece_starts[0]]
    )
    flat_input = layer_input[0]
    flat_grad = grad_out[0]
    q_width, kv_width = w_query.shape[1], w_key.shape[1]
    rows_here = w_query.shape[0]
    quarter = rows_here * groups

    weight_block = jnp.concatenate(
        [
            w_query,
            w_key,
            w_value,
            w_out.T,
            attn_norm[:, None],
            moe_norm[:, None],
            jnp.zeros((rows_here, LANES - 2), BF16),
        ],
        axis=1,
    )
    own_input = lax.dynamic_slice_in_dim(flat_input, side * half, half, 0)
    local_experts = expert_weights.shape[0] // 2
    core = shard % 2


    def experts_of(which, m):
        start = (which * local_experts, m, 0, 0)
        size = (local_experts, 1) + expert_weights.shape[2:]
        return lax.dynamic_slice(expert_weights, start, size)[:, 0]

    mine = [experts_of(core, m) for m in range(3)]
    given = [experts_of(1 - core, m) for m in range(3)]

    index = jnp.arange(groups * tokens, dtype=jnp.int32)
    positions = (index ^ (side * half).astype(jnp.int32)).astype(F32)
    lane = jnp.arange(LANES, dtype=jnp.int32)
    step = (lane % (HEAD_DIM // 2)).astype(F32)
    angles = positions[:, None] * (1.0 / 10000.0 ** (step * 2.0 / HEAD_DIM))[None, :]
    cos_table = jnp.cos(angles)
    sin_table = jnp.sin(angles) * jnp.where(lane % HEAD_DIM < HEAD_DIM // 2, -1.0, 1.0)[None, :]

    gate_high = gate_values[0].astype(BF16)
    gate_low = (gate_values[0] - gate_high.astype(F32)).astype(BF16)
    grad_block = jnp.concatenate(
        [
            flat_grad,
            expert_ids[0].astype(BF16),
            slot_ids[0].astype(BF16),
            gate_high,
            gate_low,
            jnp.zeros((tokens, LANES - 4 * TOPK), BF16),
        ],
        axis=1,
    )
    grad_block = jnp.where(
        side == 0, grad_block, jnp.concatenate([grad_block[half:], grad_block[:half]], axis=0)
    )
    grad_block = jnp.broadcast_to(grad_block[None], (groups,) + grad_block.shape)

    near = [1, 3] if groups == 4 else [1]
    rest = [b for b in range(1, groups) if b not in near]
    block_0, own_input, cos_table, sin_table, grad_block, far_0, *kept = fence(
        spread(weight_block, "ctx").reshape(quarter, -1),
        own_input,
        cos_table,
        sin_table,
        grad_block,
        swap(mine[0], "shard", 2),
        *mine,
        *given,
        *[swap(own_input, "ctx", b) for b in near],
    )
    mine, given = kept[:3], kept[3:6]
    input_at = dict(zip(near, kept[6:]))
    block_0, block_2, *kept = fence(
        block_0,
        swap(block_0, "shard", 2),
        *[swap(input_at[b], "tp", 1) for b in near],
        *[swap(own_input, "ctx", b) for b in rest],
    )
    crossed = dict(zip(near, kept[: len(near)]))
    input_at.update(dict(zip(rest, kept[len(near) :])))
    grads_own = lax.all_to_all(after(grad_block, block_2), "ctx", 0, 0, tiled=True)
    block_0, block_1, block_2, block_3, far_1, taken_0, *kept = fence(
        block_0,
        swap(block_0, "shard", 1),
        block_2,
        swap(block_2, "shard", 1),
        swap(after(mine[1], block_2), "shard", 2),
        swap(after(given[0], block_2), "shard", 1),
        *[swap(input_at[b], "tp", 1) for b in rest],
    )
    crossed.update(dict(zip(rest, kept)))
    pieces = [block_0, block_1, block_2, block_3]
    others = [v for b in range(1, groups) for v in (input_at[b], crossed[b])]

    normed_all, queries, kv_all, gains = front(
        scalars, flat_input, others, pieces, cos_table, sin_table, (q_width, kv_width)
    )
    mixed, lse, attention_own, attention_send = attend(
        scalars, queries, kv_all, pieces, piece_count
    )
    attention_send, far_2, far_3, taken_1 = fence(
        attention_send,
        swap(after(mine[2], block_1), "shard", 2),
        swap(after(taken_0, block_1), "shard", 2),
        swap(after(given[1], block_1), "shard", 1),
    )
    residual, normed_two = second_norm(
        scalars, flat_input, attention_own, swap(attention_send, "tp", 1), gains
    )

    pairs = [[0, 2], [1, 3]] if groups == 4 else [[b, b + 1] for b in range(0, groups, 2)]
    soon = [0, pairs[0][1], pairs[1][0]]
    normed_two, crossed_0, far_4, taken_2, *arrived = fence(
        normed_two,
        swap(normed_two, "tp", 1),
        swap(after(taken_1, attention_send), "shard", 2),
        swap(after(given[2], attention_send), "shard", 1),
        *[swap(normed_two, "ctx", b) for b in soon[1:]],
    )
    tokens_at = dict(zip(soon, [normed_two, *arrived]))
    late = [b for b in range(groups) if b not in soon]
    grads_own, far_5, *arrived = fence(
        grads_own,
        swap(taken_2, "shard", 2),
        *[swap(tokens_at[b], "tp", 1) for b in soon[1:]],
        *[swap(normed_two, "ctx", b) for b in late],
    )
    crossed_at = dict(zip(soon, [crossed_0, *arrived[:2]]))
    tokens_at.update(dict(zip(late, arrived[2:])))
    crossed_1 = crossed_at[soon[1]]
    arrived_1 = tokens_at[soon[1]]
    grads_in = [grads_own, swap(grads_own, "shard", 1)]
    taken = [taken_0, taken_1, taken_2]
    expert_pieces = [*mine, *taken, far_0, far_1, far_2, far_3, far_4, far_5]
    rows_own = jnp.stack(
        [jnp.stack([normed_two, crossed_0]), jnp.stack([arrived_1, crossed_1])]
    )
    rows_in = [rows_own, swap(rows_own, "shard", 1)]

    def summed(own, got, part):
        return own[:, part].astype(F32) + got[:, part].astype(F32)

    low, high = slice(0, half), slice(half, tokens)
    row_sets, grad_sets, hidden_sets = [], [], []
    norm_parts, out_parts, out_sets = {}, {}, []
    waiting = None
    order = scalars
    for n, pair in enumerate(pairs):
        own, mate, out_own, out_mate, hiddens, rows, grads = experts(
            order, pair, rows_in, grads_in, expert_pieces
        )
        row_sets.append(rows)
        grad_sets.append(grads)
        hidden_sets.append(hiddens)
        out_sets.append((pair, out_own, out_mate))
        last = n + 1 == len(pairs)
        if not last:
            later = pairs[n + 1]
            wanted = [b for b in later if b not in crossed_at]
            own, mate, *arrived = fence(own, mate, *[swap(tokens_at[b], "tp", 1) for b in wanted])
            crossed_at.update(dict(zip(wanted, arrived)))
        if waiting is not None:
            own, mate, crossed = fence(own, mate, waiting[3])
            old_pair, kept_own, got, _ = waiting
            kept = summed(kept_own, got, low) + crossed.astype(F32)
            for i, b in enumerate(old_pair):
                norm_parts[b] = kept[i] if b == 0 else swap(kept[i].astype(BF16), "ctx", b)
        if not last:
            rows_own = jnp.stack([jnp.stack([tokens_at[b], crossed_at[b]]) for b in later])
            rows_in = [rows_own, swap(rows_own, "shard", 1)]
        got = swap(mate, "shard", 1)
        sent = summed(own, got, high).astype(BF16)
        waiting = (pair, own, got, swap(sent, "tp", 1))
        order = after(scalars, sent)

    hidden_sets[-1] = after(hidden_sets[-1], sent)
    pair, own, got, crossed = waiting
    early = [b for b in norm_parts if b > 0]
    mates = [swap(after(s[2], sent), "shard", 1) for s in out_sets[:-1]]
    keep_0, keep_1, *arrived = fence(
        *expert_weight_grads(row_sets, grad_sets, hidden_sets, quarter),
        crossed,
        *[norm_parts[b] for b in early],
        *mates,
    )
    fars = len(arrived) - 1 - len(early) - len(mates)
    far_sent, crossed, arrived = arrived[:fars], arrived[fars], arrived[fars + 1 :]
    far_got = []

    def send_far(count, *ready):
        start = len(far_got)
        got = [swap(after(v, *ready), "shard", 2) for v in far_sent[start : start + count]]
        far_got.extend(got)
        return got

    def keep_far(got):
        far_got[len(far_got) - len(got) :] = got

    norm_parts.update(dict(zip(early, arrived)))
    mates = arrived[len(early) :]
    kept = summed(own, got, low) + crossed.astype(F32)
    for i, b in enumerate(pair):
        norm_parts[b] = swap(kept[i].astype(BF16), "ctx", b)

    outs = [(s[0], after(s[1], kept), m) for s, m in zip(out_sets, mates)]
    out_crossed = [swap(summed(own, got, high).astype(BF16), "tp", 1) for _, own, got in outs]
    out_last = swap(after(out_sets[-1][2], kept), "shard", 1)
    sending = send_far(1, crossed)
    residual, out_last, *arrived = fence(
        residual, out_last, *[norm_parts[b] for b in range(groups)], *sending, *out_crossed
    )
    keep_far(arrived[groups : groups + len(sending)])
    out_crossed = arrived[groups + len(sending) :]
    arrived = arrived[:groups]
    residual_grad, branch_own, gain_row = middle_grad(
        scalars, arrived, residual, flat_grad, gains
    )
    sending = send_far(1, out_last)
    branch_own, branch_crossed, *sending = fence(branch_own, swap(branch_own, "tp", 1), *sending)
    keep_far(sending)
    branch = [branch_own, branch_crossed]
    for (pair, own, got), crossed in zip(outs, out_crossed):
        kept = summed(after(own, branch_own), got, low) + crossed.astype(F32)
        for i, b in enumerate(pair):
            value = kept[i]
            out_parts[b] = value if b == 0 else swap(fence(value.astype(BF16))[0], "ctx", b)
    pair, own, _ = out_sets[-1]
    own = after(own, branch_own)
    out_crossed = swap(summed(own, out_last, high).astype(BF16), "tp", 1)

    def natural(own):
        other = swap(own, "tp", 1)
        return jnp.where(
            side == 0,
            jnp.concatenate([own, other], axis=0),
            jnp.concatenate([other, own], axis=0),
        )[None]

    dq, dkv_parts = attend_grad(
        scalars, branch, queries, kv_all, lse, pieces, cos_table, sin_table, piece_count
    )
    sending = send_far(1, branch_crossed)
    dq, dkv_parts, out_crossed, *sending = fence(dq, dkv_parts, out_crossed, *sending)
    keep_far(sending)

    kept = summed(own, out_last, low) + out_crossed.astype(F32)
    for i, b in enumerate(pair):
        out_parts[b] = swap(fence(kept[i].astype(BF16))[0], "ctx", b)
    weight_parts = qkv_grads(scalars, normed_all, dq, dkv_parts, quarter)
    out_grad_parts = out_grads(scalars, branch, after(mixed, weight_parts[0]), gain_row, quarter)
    weight_kept, weight_passed = over_mate(weight_parts)
    out_kept, out_passed = over_mate(out_grad_parts)
    sending = send_far(1, dq)
    moved = [b for b in range(1, groups)]
    dkv, weight_kept, weight_got, out_kept, out_passed, *arrived = fence(
        lax.all_to_all(
            dkv_parts.reshape(groups, tokens, 2 * kv_width), "ctx", 0, 0, tiled=True
        ),
        weight_kept,
        swap(weight_passed, "shard", 2),
        out_kept,
        out_passed,
        *[out_parts[b] for b in moved],
        *sending,
    )
    out_parts.update(dict(zip(moved, arrived)))
    keep_far(arrived[len(moved) :])

    normed_own, normed_send = back(scalars, dq, dkv, pieces)
    input_half = last_grad(
        scalars, flat_input, normed_own, swap(normed_send, "tp", 1), residual_grad, gains
    )
    sending = send_far(len(far_sent), dkv)
    weight_grad, out_got, input_half, out_kept, *sending = fence(
        over_ctx(weight_kept, weight_got),
        swap(out_passed, "shard", 2),
        input_half,
        out_kept,
        *sending,
    )
    keep_far(sending)
    input_grad = natural(input_half)
    out_sum = after(residual, dkv)
    for b in range(groups):
        out_sum = out_sum + out_parts[b].astype(F32)
    output = natural(out_sum.astype(BF16))
    weight_grad = jnp.sum(weight_grad.astype(F32), axis=0)
    query_grad = weight_grad[:, :q_width]
    key_grad = weight_grad[:, q_width : q_width + kv_width]
    value_grad = weight_grad[:, q_width + kv_width :]
    out_grad = jnp.sum(over_ctx(out_kept, out_got).astype(F32), axis=0)
    moe_sum = out_grad[:, q_width]
    moe_norm_grad = moe_sum + swap(moe_sum, "tp", 1)
    out_grad = out_grad[:, :q_width].T

    got = [v[k] for v in far_got for k in range(v.shape[0])]
    grads_0, grads_1 = [], []
    for e in range(local_experts):
        blocks = [v.astype(F32) for v in got[6 * e : 6 * e + 6]]
        grads_0.append(keep_0[e] + jnp.stack(blocks[:3]))
        grads_1.append((keep_1[e] + jnp.stack(blocks[3:])).astype(BF16))
    grad_0 = jnp.stack(grads_0)
    grad_1 = swap(jnp.stack(grads_1), "shard", 1).astype(F32)
    expert_grad = jnp.where(
        core == 0,
        jnp.concatenate([grad_0, grad_1], axis=0),
        jnp.concatenate([grad_1, grad_0], axis=0),
    )
    attn_sum = (
        jnp.sum(w_query.astype(F32) * query_grad, axis=1)
        + jnp.sum(w_key.astype(F32) * key_grad, axis=1)
        + jnp.sum(w_value.astype(F32) * value_grad, axis=1)
    )
    attn_norm_grad = (attn_sum + swap(attn_sum, "tp", 1)) / attn_norm.astype(F32)
    return (
        output,
        input_grad,
        attn_norm_grad,
        query_grad,
        key_grad,
        value_grad,
        out_grad,
        moe_norm_grad,
        expert_grad,
    )


def solution(mesh):
    in_specs = (
        P("shard", "ctx", None),
        P(("shard", "ctx")),
        P(("shard", "ctx"), "tp"),
        P(("shard", "ctx"), "tp"),
        P(("shard", "ctx"), "tp"),
        P("tp", ("shard", "ctx")),
        P(("shard", "ctx")),
        P("ctx", None, "shard", "tp"),
        P("shard", "ctx", None),
        P("shard", "ctx", None),
        P("shard", "ctx", None),
        P("shard", None),
        P("shard", "ctx", None),
    )
    out_specs = (
        P("shard", "ctx", None),
        P("shard", "ctx", None),
        P(("shard", "ctx")),
        P(("shard", "ctx"), "tp"),
        P(("shard", "ctx"), "tp"),
        P(("shard", "ctx"), "tp"),
        P("tp", ("shard", "ctx")),
        P(("shard", "ctx")),
        P("ctx", None, "shard", "tp"),
    )
    return jax.shard_map(local, mesh=mesh, in_specs=in_specs, out_specs=out_specs, check_vma=False)
```

time: 470 us -> 401 us (0.85)
  blocking collectives: 60.4 us -> 0 us
  waiting for transfers between devices: 173 us -> 129 us
  local copies, waits for them, and re-layouts: 16.6 us -> 58.5 us
  Pallas kernels: 115 us -> 86.1 us
  starting transfers between devices: 65.6 us -> 82.5 us
    all_to_all x3 -> x0, blocking collectives: 60.4 us -> none  [spread(): return lax.all_to_all(copies, axis, 0, 0, tiled=True)]
    all_to_all x2 -> x1, waiting for transfers between devices: 29.8 us -> 5.78 us  [spread(): return lax.all_to_all(copies, axis, 0, 0, tiled=True)]
    unnamed x128 -> x261, local copies, waits for them, and re-layouts: 7.58 us -> 31.2 us
    ppermute x69 -> x59, starting transfers between devices: 38.7 us -> 58.8 us  [swap(): return lax.ppermute(value, axis, [(i, i ^ distance) for i in range(size)])]
    pallas_call x8 -> x6, Pallas kernels: 76.1 us -> 58.4 us  [the longest x2 32.6 us: experts(): pl.pallas_call(body, out_shape=[sums] * 4 + [sds((local, rows_each, 3 * h...]
    ppermute x69 -> x59, waiting for transfers between devices: 137 us -> 123 us  [swap(): return lax.ppermute(value, axis, [(i, i ^ distance) for i in range(size)])]
    another operation x0 -> x5, local copies, waits for them, and re-layouts: none -> 9.57 us  [the longest x4 7.87 us: local(): grads_1.append((keep_1[e] + jnp.stack(blocks[3:])).astype(BF16))]
    convert_element_type x24 -> x11, other arithmetic: 18.3 us -> 11.4 us  [the longest x2 3.74 us: over_mate(): return (own + got[0].astype(F32), (far + got[1].astype(F32)).astype(BF16))]
  transfers between devices with their start and end apart: 75 -> 64, of which waited for: 18 -> 28; matrix products, arithmetic and copies ran while one was open for 8% -> 13% of each run, Pallas kernels for 23% -> 21%
where the time goes in v2:
time: 401 us; the launch traced here: 397 us
  waiting for transfers between devices  129 us (32%)
  Pallas kernels  86.1 us (21%)
  starting transfers between devices  82.5 us (21%)
  local copies, waits for them, and re-layouts  58.5 us (15%)
  other arithmetic  37.3 us (9%)
    ppermute x59, waiting for transfers between devices, swap(): return lax.ppermute(value, axis, [(i, i ^ distance) for i in range(size)])  123 us
    ppermute x59, starting transfers between devices, swap(): return lax.ppermute(value, axis, [(i, i ^ distance) for i in range(size)])  58.8 us
    pallas_call x2, Pallas kernels, experts(): pl.pallas_call(body, out_shape=[sums] * 4 + [sds((local, rows_each, 3 * h...  32.6 us
    unnamed x261, local copies, waits for them, and re-layouts  31.2 us
    pallas_call x1, Pallas kernels, expert_weight_grads(): pl.pallas_call(body, out_shape=[sds((local, 3, quarter, hidden), F32)] *...  12.6 us
    pallas_call x1, Pallas kernels, attend_grad(): pl.pallas_call(body, out_shape=[sds((tokens, q_width), BF16), sds((length...  12.3 us
    all_to_all x2, starting transfers between devices, over_ctx(): lax.all_to_all(total.reshape(groups, rows, total.shape[1]), 'ctx', 0, 0,...  11 us
    pallas_call x1, Pallas kernels, attend(): pl.pallas_call(body, out_shape=[sds((tokens, q_width), BF16), sds((tokens...  10.3 us
  transfers between devices with their start and end apart: 64, of which 28 were waited for; matrix products, arithmetic and copies ran while one was open for 13% of the time, Pallas kernels for 21%

profile of v2, /device:TPU:0, one launch (start us, length us, event | category | flops | bytes accessed | tf_op | source)
XLA Modules:
  0.0 396.5 jit_solution(17419549398622731700)
XLA Ops:
  2.3 5.0 %collective-permute-start.2 = (bf16[128,1024]{1,0:T(8,128)(2,1)}, bf16[128,1024]{1,0:T(8,128)(2,1)}, u32[]{:S(2)}, u32[]{:S(2)}) collective-permute-start(bf16[128,1024]{1,0:T(8,128)(2,1)} %dynamic-slice_bitcast_fusion.6), channel_id=1, source_target_pairs={{0,6},{2,4},{4,2},{6,0},{1,7},{3,5},{5,3},{7,1},{8,14},{10,12},{12... | collective-permute-start | bytes 786440 | tf_op jit(solution)/shard_map/ppermute | solution.py:24
  31.1 5.8 %all-to-all-done = bf16[4,64,1664]{2,1,0:T(8,128)(2,1)S(1)} async-done(((bf16[4,64,1664]{2,1,0:T(8,128)(2,1)}), bf16[4,64,1664]{2,1,0:T(8,128)(2,1)S(1)}, u32[]{:S(2)}, u32[]{:S(2)}) %all-to-all-start) | async-done | bytes 852000 | tf_op jit(solution)/shard_map/all_to_all | solution.py:30
  43.4 11.4 %collective-permute-done.6.rest_2_ = bf16[128,1024]{1,0:T(8,128)(2,1)S(1)} collective-permute-done((bf16[128,1024]{1,0:T(8,128)(2,1)}, bf16[128,1024]{1,0:T(8,128)(2,1)S(1)}, u32[]{:S(2)}, u32[]{:S(2)}) %collective-permute-start.6) | collective-permute-done | bytes 262176 | tf_op jit(solution)/shard_map/ppermute | solution.py:24
  59.9 5.0 %all-to-all-start.1 = ((bf16[4,256,1152]{2,1,0:T(8,128)(2,1)}), bf16[4,256,1152]{2,1,0:T(8,128)(2,1)}, u32[]{:S(2)}, u32[]{:S(2)}) async-start(bf16[4,256,1152]{2,1,0:T(8,128)(2,1)} %broadcast_in_dim.41), calls=%async_computation.1 | async-start | bytes 4718592 | tf_op jit(solution)/shard_map/all_to_all | solution.py:926
  68.5 7.2 %collective-permute-done.11.rest_3_ = bf16[128,1024]{1,0:T(8,128)(2,1)S(1)} collective-permute-done((bf16[128,1024]{1,0:T(8,128)(2,1)S(1)}, bf16[128,1024]{1,0:T(8,128)(2,1)S(1)}, u32[]{:S(2)}, u32[]{:S(2)}) %collective-permute-start.11) | collective-permute-done | bytes 262176 | tf_op jit(solution)/shard_map/ppermute | solution.py:24
  75.7 3.9 collective-permute-done.9.refs_11_
  84.7 8.9 %front.1 = (bf16[1024,1024]{1,0:T(8,128)(2,1)}, bf16[256,512]{1,0:T(8,128)(2,1)}, bf16[1024,512]{1,0:T(8,128)(2,1)}, f32[8,1024]{1,0:T(8,128)}) custom-call(s32[4]{0:T(128)} %pad_add_fusion.sc, bf16[256,1024]{1,0:T(8,128)(2,1)} %bitcast.164, bf16[128,1024]{1,0:T(8,128)(2,1)} %collective-permute-done.1.rest_0_, bf16[128,1024]{1,0:T(8,128)(2,1)} %copy-done.119, ...), custom_call_target="tpu_custom_call" | custom-call | flops 1342177280 | bytes 7340032 | tf_op jit(solution)/shard_map/front/pallas_call | solution.py:152
  93.7 10.3 %attend.1 = (bf16[256,512]{1,0:T(8,128)(2,1)}, f32[256,512]{1,0:T(8,128)}, f32[128,1024]{1,0:T(8,128)}, bf16[128,1024]{1,0:T(8,128)(2,1)}) custom-call(s32[4]{0:T(128)} %pad_add_fusion.sc, bf16[256,512]{1,0:T(8,128)(2,1)} %get-tuple-element.181.q_ref, bf16[1024,512]{1,0:T(8,128)(2,1)} %get-tuple-element.182.k_ref.v_ref, ...), custom_call_target="tpu_custom_call" | custom-call | flops 805306368 | bytes 4194304 | tf_op jit(solution)/shard_map/attend/pallas_call | solution.py:241
  109.0 3.8 collective-permute-done.15.rec_ref
  122.0 6.4 %collective-permute-done.20 = bf16[128,1024]{1,0:T(8,128)(2,1)S(1)} collective-permute-done((bf16[128,1024]{1,0:T(8,128)(2,1)S(1)}, bf16[128,1024]{1,0:T(8,128)(2,1)S(1)}, u32[]{:S(2)}, u32[]{:S(2)}) %collective-permute-start.20) | collective-permute-done | bytes 262176 | tf_op jit(solution)/shard_map/ppermute | solution.py:24
  152.7 16.4 %experts.2 = (bf16[2,256,1024]{2,1,0:T(8,128)(2,1)S(1)}, bf16[2,256,1024]{2,1,0:T(8,128)(2,1)S(1)}, bf16[2,256,1024]{2,1,0:T(8,128)(2,1)S(1)}, bf16[2,256,1024]{...) custom-call(s32[4]{0:T(128)S(1)} %copy-done.51, ...), custom_call_target="tpu_custom_call" | custom-call | flops 8053063680 | bytes 18874368 | tf_op jit(solution)/shard_map/experts/pallas_call | solution.py:412
  175.3 16.2 %experts.3 = (bf16[2,256,1024]{2,1,0:T(8,128)(2,1)S(1)}, bf16[2,256,1024]{2,1,0:T(8,128)(2,1)S(1)}, bf16[2,256,1024]{2,1,0:T(8,128)(2,1)S(1)}, bf16[2,256,1024]{...) custom-call(s32[4]{0:T(128)S(1)} %copy-done.51, ...), custom_call_target="tpu_custom_call" | custom-call | flops 8053063680 | bytes 18874368 | tf_op jit(solution)/shard_map/experts/pallas_call | solution.py:412
  198.7 12.6 %expert_weight_grads.1 = (f32[4,3,256,256]{3,2,1,0:T(8,128)}, f32[4,3,256,256]{3,2,1,0:T(8,128)}, bf16[6,256,256]{2,1,0:T(8,128)(2,1)}, bf16[2,256,256]{2,1,0:T(...) custom-call(bf16[4,384,1024]{2,1,0:T(8,128)(2,1)} %copy-done.68, ...), custom_call_target="tpu_custom_call" | custom-call | flops 4831838208 | bytes 26738688 | tf_op jit(solution)/shard_map/expert_weight_grads/pallas_call | solution.py:487
  219.4 8.9 %collective-permute-done.37.refs_3_ = bf16[128,1024]{1,0:T(8,128)(2,1)S(1)} collective-permute-done((bf16[128,1024]{1,0:T(8,128)(2,1)S(1)}, bf16[128,1024]{1,0:T(8,128)(2,1)S(1)}, u32[]{:S(2)}, u32[]{:S(2)}) %collective-permute-start.37) | collective-permute-done | bytes 262176 | tf_op jit(solution)/shard_map/ppermute | solution.py:24
  228.3 4.1 %collective-permute-done.36.refs_1_ = bf16[128,1024]{1,0:T(8,128)(2,1)S(1)} collective-permute-done((bf16[128,1024]{1,0:T(8,128)(2,1)S(1)}, bf16[128,1024]{1,0:T(8,128)(2,1)S(1)}, u32[]{:S(2)}, u32[]{:S(2)}) %collective-permute-start.36) | collective-permute-done | bytes 262176 | tf_op jit(solution)/shard_map/ppermute | solution.py:24
  240.3 4.5 %collective-permute-done.41 = bf16[2,256,256]{2,1,0:T(8,128)(2,1)S(1)} collective-permute-done((bf16[2,256,256]{2,1,0:T(8,128)(2,1)S(1)}, bf16[2,256,256]{2,1,0:T(8,128)(2,1)S(1)}, u32[]{:S(2)}, u32[]{:S(2)}) %collective-permute-start.41) | collective-permute-done | bytes 262176 | tf_op jit(solution)/shard_map/ppermute | solution.py:24
  259.3 12.3 %attend_grad.1 = (bf16[256,512]{1,0:T(8,128)(2,1)S(1)}, bf16[1024,512]{1,0:T(8,128)(2,1)S(1)}) custom-call(s32[4]{0:T(128)S(1)} %copy-done.51, bf16[128,1024]{1,0:T(8,128)(2,1)S(1)} %copy-done.44, bf16[128,1024]{1,0:T(8,128)(2,1)S(1)} %copy-done.47, bf16[256,512]{1,0:T(8,128)(2,1)S(1)} %copy-done.21, bf16[1024,512]{1,0:T(8,128)(2,1)S(1)} %copy-done.2, ...), custom_call_target="tpu_custom_call" | custom-call | flops 1610612736 | bytes 5242880 | tf_op jit(solution)/shard_map/attend_grad/pallas_call | solution.py:612
  276.6 4.3 %all-to-all-start.2 = ((bf16[4,256,512]{2,1,0:T(8,128)(2,1)}), bf16[4,256,512]{2,1,0:T(8,128)(2,1)}, u32[]{:S(2)}, u32[]{:S(2)}) async-start(bf16[4,256,512]{2,1,0:T(8,128)(2,1)} %bitcast.170), calls=%async_computation.2 | async-start | bytes 2097152 | tf_op jit(solution)/shard_map/all_to_all | solution.py:1101
  299.5 25.3 %collective-permute-done.48 = bf16[128,1024]{1,0:T(8,128)(2,1)S(1)} collective-permute-done((bf16[128,1024]{1,0:T(8,128)(2,1)S(1)}, bf16[128,1024]{1,0:T(8,128)(2,1)S(1)}, u32[]{:S(2)}, u32[]{:S(2)}) %collective-permute-start.48) | collective-permute-done | bytes 262176 | tf_op jit(solution)/shard_map/ppermute | solution.py:24
  328.6 6.2 %all-to-all-start.3 = ((bf16[4,64,1024]{2,1,0:T(8,128)(2,1)}), bf16[4,64,1024]{2,1,0:T(8,128)(2,1)}, u32[]{:S(2)}, u32[]{:S(2)}) async-start(bf16[4,64,1024]{2,1,0:T(8,128)(2,1)} %bitcast.173), calls=%async_computation.3 | async-start | bytes 1048576 | tf_op jit(solution)/shard_map/all_to_all | solution.py:742
  351.2 9.4 %collective-permute-done.52 = bf16[256,640]{1,0:T(8,128)(2,1)S(1)} collective-permute-done((bf16[256,640]{1,0:T(8,128)(2,1)S(1)}, bf16[256,640]{1,0:T(8,128)(2,1)S(1)}, u32[]{:S(2)}, u32[]{:S(2)}) %collective-permute-start.52) | collective-permute-done | bytes 327712 | tf_op jit(solution)/shard_map/ppermute | solution.py:24
  370.5 4.8 %all-to-all-start.4 = ((bf16[4,64,640]{2,1,0:T(8,128)(2,1)}), bf16[4,64,640]{2,1,0:T(8,128)(2,1)S(1)}, u32[]{:S(2)}, u32[]{:S(2)}) async-start(bf16[4,64,640]{2,1,0:T(8,128)(2,1)} %bitcast.52), calls=%async_computation.4 | async-start | bytes 655360 | tf_op jit(solution)/shard_map/all_to_all | solution.py:742
  379.9 4.8 %collective-permute-done.55 = bf16[128,1024]{1,0:T(8,128)(2,1)S(1)} collective-permute-done((bf16[128,1024]{1,0:T(8,128)(2,1)S(1)}, bf16[128,1024]{1,0:T(8,128)(2,1)S(1)}, u32[]{:S(2)}, u32[]{:S(2)}) %collective-permute-start.55) | collective-permute-done | bytes 262176 | tf_op jit(solution)/shard_map/ppermute | solution.py:24
  392.7 3.6 broadcast_select_fusion
  (448 shorter events, 192.4 us)
Async XLA Ops:
  2.3 27.4 %collective-permute-start.2 = (bf16[128,1024]{1,0:T(8,128)(2,1)}, bf16[128,1024]{1,0:T(8,128)(2,1)}, u32[]{:S(2)}, u32[]{:S(2)}) collective-permute-start(bf16[128,1024]{1,0:T(8,128)(2,1)} %dynamic-slice_bitcast_fusion.6), channel_id=1, source_target_pairs={{0,6},{2,4},{4,2},{6,0},{1,7},{3,5},{5,3},{7,1},{8,14},{10,12},{12... | collective-permute-start | bytes 786440 | tf_op jit(solution)/shard_map/ppermute | solution.py:24
  7.4 22.3 %collective-permute-start.1 = (bf16[128,1024]{1,0:T(8,128)(2,1)}, bf16[128,1024]{1,0:T(8,128)(2,1)}, u32[]{:S(2)}, u32[]{:S(2)}) collective-permute-start(bf16[128,1024]{1,0:T(8,128)(2,1)} %dynamic-slice_bitcast_fusion.6), channel_id=1, source_target_pairs={{0,2},{2,0},{4,6},{6,4},{1,3},{3,1},{5,7},{7,5},{8,10},{10,8},{12,... | collective-permute-start | bytes 786440 | tf_op jit(solution)/shard_map/ppermute | solution.py:24
  10.9 26.0 %all-to-all-start = ((bf16[4,64,1664]{2,1,0:T(8,128)(2,1)}), bf16[4,64,1664]{2,1,0:T(8,128)(2,1)S(1)}, u32[]{:S(2)}, u32[]{:S(2)}) async-start(bf16[4,64,1664]{2,1,0:T(8,128)(2,1)} %broadcast_in_dim.38), calls=%async_computation | async-start | bytes 1703936 | tf_op jit(solution)/shard_map/all_to_all | solution.py:30
  39.9 20.0 %collective-permute-start.3 = (bf16[256,1664]{1,0:T(8,128)(2,1)S(1)}, bf16[256,1664]{1,0:T(8,128)(2,1)S(1)}, u32[]{:S(2)}, u32[]{:S(2)}) collective-permute-start(bf16[256,1664]{1,0:T(8,128)(2,1)S(1)} %bitcast.158), channel_id=1, source_target_pairs={{0,16},{8,24},{16,0},{24,8},{1,17},{9,25},{17,1},{25,9},{2,18},{10... | collective-permute-start | bytes 2555912 | tf_op jit(solution)/shard_map/ppermute | solution.py:24
  59.9 84.6 %all-to-all-start.1 = ((bf16[4,256,1152]{2,1,0:T(8,128)(2,1)}), bf16[4,256,1152]{2,1,0:T(8,128)(2,1)}, u32[]{:S(2)}, u32[]{:S(2)}) async-start(bf16[4,256,1152]{2,1,0:T(8,128)(2,1)} %broadcast_in_dim.41), calls=%async_computation.1 | async-start | bytes 4718592 | tf_op jit(solution)/shard_map/all_to_all | solution.py:926
  81.4 22.6 %collective-permute-start.12 = (bf16[4,256,256]{2,1,0:T(8,128)(2,1)S(1)}, bf16[4,256,256]{2,1,0:T(8,128)(2,1)}, u32[]{:S(2)}, u32[]{:S(2)}) collective-permute-start(bf16[4,256,256]{2,1,0:T(8,128)(2,1)S(1)} %get-tuple-element.186.refs_6_), channel_id=1, source_target_pairs={{0,16},{8,24},{16,0},{24,8},{1,17},{9,25},{17,1},{25,9},{2,18},{10... | collective-permute-start | bytes 1572872 | tf_op jit(solution)/shard_map/ppermute | solution.py:24
  82.9 21.1 %collective-permute-start.14 = (bf16[4,256,256]{2,1,0:T(8,128)(2,1)}, bf16[4,256,256]{2,1,0:T(8,128)(2,1)}, u32[]{:S(2)}, u32[]{:S(2)}) collective-permute-start(bf16[4,256,256]{2,1,0:T(8,128)(2,1)} %get-tuple-element.190), channel_id=1, source_target_pairs={{0,8},{8,0},{16,24},{24,16},{1,9},{9,1},{17,25},{25,17},{2,10},{10... | collective-permute-start | bytes 1572872 | tf_op jit(solution)/shard_map/ppermute | solution.py:24
  82.9 23.0 %collective-permute-start.13 = (bf16[4,256,256]{2,1,0:T(8,128)(2,1)}, bf16[4,256,256]{2,1,0:T(8,128)(2,1)}, u32[]{:S(2)}, u32[]{:S(2)}) collective-permute-start(bf16[4,256,256]{2,1,0:T(8,128)(2,1)} %collective-permute-done.10.refs_7_), channel_id=1, source_target_pairs={{0,16},{8,24},{16,0},{24,8},{1,17},{9,25},{17,1},{25,9},{2,18},{10... | collective-permute-start | bytes 1572872 | tf_op jit(solution)/shard_map/ppermute | solution.py:24
  147.3 23.3 %collective-permute-start.27 = (bf16[128,1024]{1,0:T(8,128)(2,1)S(1)}, bf16[128,1024]{1,0:T(8,128)(2,1)S(1)}, u32[]{:S(2)}, u32[]{:S(2)}) collective-permute-start(bf16[128,1024]{1,0:T(8,128)(2,1)S(1)} %collective-permute-done.24), channel_id=1, source_target_pairs={{0,1},{1,0},{2,3},{3,2},{4,5},{5,4},{6,7},{7,6},{8,9},{9,8},{10,11... | collective-permute-start | bytes 786440 | tf_op jit(solution)/shard_map/ppermute | solution.py:24
  173.5 19.5 %collective-permute-start.30 = (bf16[2,128,1024]{2,1,0:T(8,128)(2,1)S(1)}, bf16[2,128,1024]{2,1,0:T(8,128)(2,1)S(1)}, u32[]{:S(2)}, u32[]{:S(2)}) collective-permute-start(bf16[2,128,1024]{2,1,0:T(8,128)(2,1)S(1)} %add_convert_fusion.5), channel_id=1, source_target_pairs={{0,1},{1,0},{2,3},{3,2},{4,5},{5,4},{6,7},{7,6},{8,9},{9,8},{10,11... | collective-permute-start | bytes 1572872 | tf_op jit(solution)/shard_map/ppermute | solution.py:24
  215.7 20.3 %collective-permute-start.35 = (bf16[2,256,1024]{2,1,0:T(8,128)(2,1)}, bf16[2,256,1024]{2,1,0:T(8,128)(2,1)S(1)}, u32[]{:S(2)}, u32[]{:S(2)}) collective-permute-start(bf16[2,256,1024]{2,1,0:T(8,128)(2,1)} %get-tuple-element.246), channel_id=1, source_target_pairs={{0,8},{8,0},{16,24},{24,16},{1,9},{9,1},{17,25},{25,17},{2,10},{10... | collective-permute-start | bytes 3145736 | tf_op jit(solution)/shard_map/ppermute | solution.py:24
  215.8 20.2 %collective-permute-start.38 = (bf16[6,256,256]{2,1,0:T(8,128)(2,1)}, bf16[6,256,256]{2,1,0:T(8,128)(2,1)S(1)}, u32[]{:S(2)}, u32[]{:S(2)}) collective-permute-start(bf16[6,256,256]{2,1,0:T(8,128)(2,1)} %get-tuple-element.249), channel_id=1, source_target_pairs={{0,16},{8,24},{16,0},{24,8},{1,17},{9,25},{17,1},{25,9},{2,18},{10... | collective-permute-start | bytes 2359304 | tf_op jit(solution)/shard_map/ppermute | solution.py:24
  247.3 24.4 %collective-permute-start.42 = (bf16[2,128,1024]{2,1,0:T(8,128)(2,1)}, bf16[2,128,1024]{2,1,0:T(8,128)(2,1)}, u32[]{:S(2)}, u32[]{:S(2)}) collective-permute-start(bf16[2,128,1024]{2,1,0:T(8,128)(2,1)} %add_convert_fusion.2), channel_id=1, source_target_pairs={{0,1},{1,0},{2,3},{3,2},{4,5},{5,4},{6,7},{7,6},{8,9},{9,8},{10,11... | collective-permute-start | bytes 1572872 | tf_op jit(solution)/shard_map/ppermute | solution.py:24
  248.1 23.6 %collective-permute-start.43 = (bf16[4,256,256]{2,1,0:T(8,128)(2,1)}, bf16[4,256,256]{2,1,0:T(8,128)(2,1)}, u32[]{:S(2)}, u32[]{:S(2)}) collective-permute-start(bf16[4,256,256]{2,1,0:T(8,128)(2,1)} %get-tuple-element.270), channel_id=1, source_target_pairs={{0,16},{8,24},{16,0},{24,8},{1,17},{9,25},{17,1},{25,9},{2,18},{10... | collective-permute-start | bytes 1572872 | tf_op jit(solution)/shard_map/ppermute | solution.py:24
  276.6 49.7 %all-to-all-start.2 = ((bf16[4,256,512]{2,1,0:T(8,128)(2,1)}), bf16[4,256,512]{2,1,0:T(8,128)(2,1)}, u32[]{:S(2)}, u32[]{:S(2)}) async-start(bf16[4,256,512]{2,1,0:T(8,128)(2,1)} %bitcast.170), calls=%async_computation.2 | async-start | bytes 2097152 | tf_op jit(solution)/shard_map/all_to_all | solution.py:1101
  282.1 42.7 %collective-permute-start.48 = (bf16[128,1024]{1,0:T(8,128)(2,1)S(1)}, bf16[128,1024]{1,0:T(8,128)(2,1)S(1)}, u32[]{:S(2)}, u32[]{:S(2)}) collective-permute-start(bf16[128,1024]{1,0:T(8,128)(2,1)S(1)} %fusion.17), channel_id=1, source_target_pairs={{0,4},{2,6},{4,0},{6,2},{1,5},{3,7},{5,1},{7,3},{8,12},{10,14},{12... | collective-permute-start | bytes 786440 | tf_op jit(solution)/shard_map/ppermute | solution.py:24
  292.0 34.3 %collective-permute-start.50 = (bf16[6,256,256]{2,1,0:T(8,128)(2,1)}, bf16[6,256,256]{2,1,0:T(8,128)(2,1)}, u32[]{:S(2)}, u32[]{:S(2)}) collective-permute-start(bf16[6,256,256]{2,1,0:T(8,128)(2,1)} %get-tuple-element.287), channel_id=1, source_target_pairs={{0,16},{8,24},{16,0},{24,8},{1,17},{9,25},{17,1},{25,9},{2,18},{10... | collective-permute-start | bytes 2359304 | tf_op jit(solution)/shard_map/ppermute | solution.py:24
  295.1 31.2 %collective-permute-start.45 = (bf16[256,1024]{1,0:T(8,128)(2,1)}, bf16[256,1024]{1,0:T(8,128)(2,1)}, u32[]{:S(2)}, u32[]{:S(2)}) collective-permute-start(bf16[256,1024]{1,0:T(8,128)(2,1)} %get-tuple-element.341), channel_id=1, source_target_pairs={{0,16},{8,24},{16,0},{24,8},{1,17},{9,25},{17,1},{25,9},{2,18},{10... | collective-permute-start | bytes 1572872 | tf_op jit(solution)/shard_map/ppermute | solution.py:24
  296.8 28.0 %collective-permute-start.47 = (bf16[128,1024]{1,0:T(8,128)(2,1)S(1)}, bf16[128,1024]{1,0:T(8,128)(2,1)S(1)}, u32[]{:S(2)}, u32[]{:S(2)}) collective-permute-start(bf16[128,1024]{1,0:T(8,128)(2,1)S(1)} %get-tuple-element.370), channel_id=1, source_target_pairs={{0,2},{2,0},{4,6},{6,4},{1,3},{3,1},{5,7},{7,5},{8,10},{10,8},{12,... | collective-permute-start | bytes 786440 | tf_op jit(solution)/shard_map/ppermute | solution.py:24
  298.3 26.4 %collective-permute-start.49 = (bf16[128,1024]{1,0:T(8,128)(2,1)S(1)}, bf16[128,1024]{1,0:T(8,128)(2,1)S(1)}, u32[]{:S(2)}, u32[]{:S(2)}) collective-permute-start(bf16[128,1024]{1,0:T(8,128)(2,1)S(1)} %get-tuple-element.369), channel_id=1, source_target_pairs={{0,6},{2,4},{4,2},{6,0},{1,7},{3,5},{5,3},{7,1},{8,14},{10,12},{12... | collective-permute-start | bytes 786440 | tf_op jit(solution)/shard_map/ppermute | solution.py:24
  328.6 32.0 %all-to-all-start.3 = ((bf16[4,64,1024]{2,1,0:T(8,128)(2,1)}), bf16[4,64,1024]{2,1,0:T(8,128)(2,1)}, u32[]{:S(2)}, u32[]{:S(2)}) async-start(bf16[4,64,1024]{2,1,0:T(8,128)(2,1)} %bitcast.173), calls=%async_computation.3 | async-start | bytes 1048576 | tf_op jit(solution)/shard_map/all_to_all | solution.py:742
  334.8 25.8 %collective-permute-start.54 = (bf16[6,256,256]{2,1,0:T(8,128)(2,1)}, bf16[6,256,256]{2,1,0:T(8,128)(2,1)}, u32[]{:S(2)}, u32[]{:S(2)}) collective-permute-start(bf16[6,256,256]{2,1,0:T(8,128)(2,1)} %get-tuple-element.301), channel_id=1, source_target_pairs={{0,16},{8,24},{16,0},{24,8},{1,17},{9,25},{17,1},{25,9},{2,18},{10... | collective-permute-start | bytes 2359304 | tf_op jit(solution)/shard_map/ppermute | solution.py:24
  344.2 33.2 %collective-permute-start.51 = (bf16[128,1024]{1,0:T(8,128)(2,1)S(1)}, bf16[128,1024]{1,0:T(8,128)(2,1)}, u32[]{:S(2)}, u32[]{:S(2)}) collective-permute-start(bf16[128,1024]{1,0:T(8,128)(2,1)S(1)} %fusion.7), channel_id=1, source_target_pairs={{0,1},{1,0},{2,3},{3,2},{4,5},{5,4},{6,7},{7,6},{8,9},{9,8},{10,11... | collective-permute-start | bytes 786440 | tf_op jit(solution)/shard_map/ppermute | solution.py:24
  368.2 22.4 %collective-permute-start.58 = (bf16[4,3,256,256]{3,2,1,0:T(8,128)(2,1)}, bf16[4,3,256,256]{3,2,1,0:T(8,128)(2,1)S(1)}, u32[]{:S(2)}, u32[]{:S(2)}) collective-permute-start(bf16[4,3,256,256]{3,2,1,0:T(8,128)(2,1)} %pad_maximum_fusion), channel_id=1, source_target_pairs={{0,8},{8,0},{16,24},{24,16},{1,9},{9,1},{17,25},{25,17},{2,10},{10... | collective-permute-start | bytes 4718600 | tf_op jit(solution)/shard_map/ppermute | solution.py:24
  (169 other events, 1698.1 us)
